TPU v7x, 1024 devices: a whole 4x8x16 slice. The times are simulated.
1024 devices in a mesh: ctx: 32 (over y, x), pp: 2 (over core), tp: 16 (over z).
Axes of the slice: x: 4, y: 8, z: 16, core: 2. Of those that a mesh axis runs over, the one named last changes fastest.
Arguments:
- outgoing: bfloat16 [2, 4096, 7168], P('pp', 'ctx', 'tp'), may hold values from -6 to 6
- w_down: bfloat16 [2, 7168, 576], P('pp', 'tp'), may hold values from -0.0625 to 0.0625
- kv_gain: float32 [2, 512], P('pp'), may hold values from 0.5 to 1.5
- queries: bfloat16 [2, 4096, 64, 192], P('pp', 'ctx', 'tp'), may hold values from -160 to 160
- w_key_up: bfloat16 [2, 64, 128, 512], P('pp', 'tp'), may hold values from -0.5 to 0.5
- w_value_up: bfloat16 [2, 64, 512, 128], P('pp', 'tp'), may hold values from -0.25 to 0.25
- block_ids: int32 [64], replicated, may hold values from 0 to 63, as said below
Outputs:
- heads_out: bfloat16 [2, 4096, 8192], P('pp', 'ctx', 'tp')
Inputs may be any that keep to these rules, and one draw needn't show every extreme that they name: `block_ids`: each number appears once; index d of ctx holds the pair k and 63 - k for some k, in either order.
All inputs are finite; a program needn't handle non-finite values.
Results may differ from a plain program's by a relative error of at most 0.02.
Values may be sent and summed in bfloat16 or wider, within the bound.
No kernel may reach another device: no remote copies, remote signals or barrier semaphores. Data moves between devices by JAX's collectives and lax.ppermute only.
A program may use at most 32 MiB of HBM per device.

v0:
```python
import jax
import jax.numpy as jnp
from jax import lax
from jax.sharding import Mesh
from jax.sharding import PartitionSpec as P

CTX = ("ctx_0", "ctx_1")


def shifted(array, axis, by):
    size = lax.axis_size(axis)
    pairs = [(i, i + by) for i in range(size) if 0 <= i + by < size]
    return lax.ppermute(array, axis, pairs)


def cut_along(array, dim, size):
    before, after = (array.shape[:dim], array.shape[dim + 1 :])
    return jnp.moveaxis(array.reshape(*before, size, -1, *after), dim, 0)


def sum_at_owner(array, axis, dim):
    size = lax.axis_size(axis)
    pieces = lax.all_to_all(cut_along(array, dim, size), axis, 0, 0, tiled=True)
    return jnp.sum(pieces, axis=0)


def sent_to_all(array, axis):
    copies = jnp.broadcast_to(array, (lax.axis_size(axis), *array.shape))
    return lax.all_to_all(copies, axis, split_axis=0, concat_axis=0, tiled=True)


def laid_out(pieces, dim):
    pieces = jnp.moveaxis(pieces, 0, dim)
    shape = pieces.shape
    return pieces.reshape(*shape[:dim], shape[dim] * shape[dim + 1], *shape[dim + 2 :])


def gather_directly(array, axis, dim):
    pieces = sent_to_all(array, axis)
    return laid_out(pieces, dim)


def gathered_by_axis(array, axes, dim):
    for axis in reversed(axes):
        array = lax.all_gather(array, axis, axis=dim, tiled=True)
    return array


def look_table(table, slot_idx):
    columns = jnp.arange(table.shape[0], dtype=jnp.int32)
    return jnp.sum(jnp.where(slot_idx[:, None] == columns[None, :], table[None, :], 0), axis=1)


def normalize(raw_latent, gain_row, latent):
    latent_part = raw_latent[:, :latent]
    mean_sq = jnp.mean(latent_part * latent_part, axis=-1, keepdims=True)
    normed = latent_part * lax.rsqrt(mean_sq + 1e-06) * gain_row
    return jnp.concatenate([normed, raw_latent[:, latent:]], axis=-1).astype(jnp.bfloat16)


def shards(outgoing, w_down, kv_gain, queries, w_key_up, w_value_up, block_ids):
    section_idx = lax.axis_index("pp")
    moved = shifted(outgoing, "pp", 1)
    section_in = jnp.where(section_idx == 0, outgoing, moved)[0]
    partial_value = jnp.dot(section_in, w_down[0], preferred_element_type=jnp.float32)
    tokens = section_in.shape[0]
    half_len = tokens // 2
    latent = w_key_up.shape[-1]
    my_index = lax.axis_index(CTX)
    token_idx = jnp.arange(tokens, dtype=jnp.int32)
    query_pos = (
        look_table(block_ids, 2 * my_index + token_idx // half_len) * half_len
        + token_idx % half_len
    )
    query = queries[0]
    heads = query.shape[1]
    nope_dim = w_key_up.shape[2]
    query_latent = jnp.einsum(
        "thd,hdc->thc", query[..., :nope_dim], w_key_up[0], preferred_element_type=jnp.float32
    ).astype(jnp.bfloat16)
    query_full = jnp.concatenate([query_latent, query[..., nope_dim:]], axis=-1).reshape(
        tokens * heads, -1
    )
    row_pos = jnp.repeat(query_pos, heads)
    score_scale = 1.0 / jnp.sqrt(jnp.float32(query.shape[-1]))
    total_rows = tokens * heads
    raw_latent = sum_at_owner(partial_value, "tp", 0)
    local_share = normalize(raw_latent, kv_gain[0], latent)
    key_rows = gather_directly(local_share, "tp", 0)
    block_rows = gathered_by_axis(key_rows, CTX, 0)
    running_max = jnp.full((total_rows,), -1e30, jnp.float32)
    row_count = block_rows.shape[0]
    rows_index = jnp.arange(row_count, dtype=jnp.int32)
    owner = rows_index // tokens
    within = rows_index % tokens
    key_pos = look_table(block_ids, 2 * owner + within // half_len) * half_len + within % half_len
    scores = jnp.dot(query_full, block_rows.T, preferred_element_type=jnp.float32) * score_scale
    visible = key_pos[None, :] <= row_pos[:, None]
    scores = jnp.where(visible, scores, jnp.float32(-1e30))
    new_max = jnp.maximum(running_max, jnp.max(scores, axis=1))
    expo = jnp.where(visible, jnp.exp(scores - new_max[:, None]), jnp.float32(0.0))
    running_sum = jnp.sum(expo, axis=1)
    weighted = jnp.dot(
        expo.astype(jnp.bfloat16), block_rows[:, :latent], preferred_element_type=jnp.float32
    )
    running_max, running_sum, weighted = (new_max, running_sum, weighted)
    attended = (weighted / running_sum[:, None]).astype(jnp.bfloat16).reshape(tokens, heads, latent)
    heads_out = jnp.einsum(
        "thc,hcv->thv", attended, w_value_up[0], preferred_element_type=jnp.float32
    )
    return heads_out.astype(jnp.bfloat16).reshape(1, tokens, -1)


def solution(mesh):
    torus = Mesh(
        mesh.devices.reshape(8, 4, mesh.shape["pp"], mesh.shape["tp"]),
        ("ctx_0", "ctx_1", "pp", "tp"),
    )
    placed = (
        P("pp", CTX, "tp"),
        P("pp", "tp", None),
        P("pp", None),
        P("pp", CTX, "tp", None),
        P("pp", "tp", None, None),
        P("pp", "tp", None, None),
        P(),
    )
    return jax.shard_map(
        shards, mesh=torus, in_specs=placed, out_specs=P("pp", CTX, "tp"), check_vma=False
    )
```

profile of v0, /device:TPU:1, one launch (start us, length us, event | category | flops | bytes accessed | tf_op | source)
XLA Modules:
  0.0 173.1 jit_solution(4996727039747953673)
XLA Ops:
  6.5 0.0 copy-start
  6.5 0.0 all-gather.2.cloned.1.call-start
  6.5 1.1 copy.29
  7.6 1.3 collective-permute-start
  8.9 14.9 %collective-permute-done = bf16[1,128,448]{2,1,0:T(8,128)(2,1)S(1)} collective-permute-done((bf16[1,128,448]{2,1,0:T(8,128)(2,1)S(1)}, bf16[1,128,448]{2,1,0:T(8,128)(2,1)S(1)}, u32[]{:S(2)}, u32[]{:S(2)}) %collective-permute-start) | collective-permute-done | bytes 114720 | tf_op jit(solution)/shard_map/ppermute | solution.py:13
  23.8 0.0 copy-done
  23.8 0.3 fusion.16
  24.1 21.8 %all_to_all.10 = f32[16,8,576]{2,1,0:T(8,128)S(1)} all-to-all(f32[16,8,576]{2,1,0:T(8,128)S(1)} %fusion.16), channel_id=1, replica_groups=mesh['ctx_0'=8,'ctx_1'=4,'pp'=2,'tp'=16] {'tp'}, dimensions={0} | all-to-all | bytes 589824 | tf_op jit(solution)/shard_map/all_to_all | solution.py:23
  45.9 0.1 multiply_reduce_fusion
  46.1 0.8 multiply_convert_fusion
  46.8 23.7 %all_to_all.11 = bf16[16,8,576]{2,1,0:T(8,128)(2,1)S(1)} all-to-all(bf16[16,8,576]{2,1,0:T(8,128)(2,1)S(1)} %broadcast_in_dim.55), channel_id=1, replica_groups=mesh['ctx_0'=8,'ctx_1'=4,'pp'=2,'tp'=16] {'tp'}, dimensions={0} | all-to-all | bytes 294912 | tf_op jit(solution)/shard_map/all_to_all | solution.py:29
  70.5 11.2 %all_gather.6 = bf16[512,576]{1,0:T(8,128)(2,1)} all-gather(bf16[128,576]{1,0:T(8,128)(2,1)S(1)} %bitcast.25), channel_id=1, replica_groups=mesh['ctx_0'=8,'ctx_1'=4,'pp'=2,'tp'=16] {'ctx_1'}, dimensions={0}, use_global_device_ids=true | all-gather | bytes 737280 | tf_op jit(solution)/shard_map/all_gather | solution.py:45
  81.7 0.0 all-gather.2.cloned.1.call-update
  81.8 0.7 select_reduce_fusion.1
  82.5 0.1 broadcast_in_dim.54
  82.6 0.1 le.16
  82.7 1.1 copy.24
  83.8 0.1 copy.26
  84.0 1.4 fusion.11
  85.4 0.8 copy.27
  86.2 0.3 reshape.104
  86.6 0.0 copy-done.2
  86.6 0.2 select_reduce_fusion
  86.8 67.1 %all-gather.2.cloned.1.call-done = bf16[4096,576]{1,0:T(8,128)(2,1)} async-done(((bf16[512,576]{1,0:T(8,128)(2,1)}), bf16[4096,576]{1,0:T(8,128)(2,1)}) %all-gather.2.cloned.1.call-update) | async-done | bytes 4718608 | tf_op jit(solution)/shard_map/all_gather | solution.py:45
  153.9 5.8 %fusion = (f32[512]{0:T(512)S(1)}, f32[512,4096]{1,0:T(8,128)S(1)}) fusion(s32[4096]{0:T(1024)S(1)} %fusion.33, s32[512]{0:T(512)S(1)} %le.16, bf16[512,576]{1,0:T(8,128)(2,1)S(1)} %reshape.104, bf16[4096,576]{1,0:T(8,128)(2,1)} %all-gather.2.cloned.1.call-done), kind=kOutput, calls=%fused_computation.2 | convolution fusion | flops 2424307200 | bytes 13717504 | tf_op jit(solution)/shard_map/dot_general | solution.py:97
  159.7 2.6 %fusion.1 = f32[512]{0:T(512)S(1)} fusion(f32[512,4096]{1,0:T(8,128)S(1)} %get-tuple-element.6, f32[512]{0:T(512)S(1)} %broadcast_maximum_fusion, s32[4096]{0:T(1024)S(1)} %fusion.33, s32[512]{0:T(512)S(1)} %le.16), kind=kLoop, calls=%fused_computation.3 | loop fusion | flops 12582400 | bytes 8411136 | tf_op jit(solution)/shard_map/reduce_sum | solution.py:102
  162.3 0.0 copy-start.1
  162.3 2.6 %divide_convert_fusion = bf16[512,512]{1,0:T(8,128)(2,1)S(1)} fusion(bf16[4096,576]{1,0:T(8,128)(2,1)S(1)} %copy-done.3, f32[512,4096]{1,0:T(8,128)S(1)} %get-tuple-element.6, f32[512]{0:T(512)S(1)} %broadcast_maximum_fusion, s32[4096]{0:T(1024)S(1)} %fusion.33, s32[512]{0:T(512)S(1)} %le.16, f32[512]{0:T(512)S(1)} %fusion.1), kind=kOutput, calls=%fused_computation.15 | convolution fusion | flops 2160590848 | bytes 13129728 | tf_op jit(solution)/shard_map/dot_general | solution.py:103
  165.0 0.1 reshape.106
  165.1 0.0 copy-done.1
  165.1 0.3 convolution_convert_fusion.1
  165.5 0.8 copy.32
  (15 shorter events, 0.2 us)
Async XLA Ops:
  6.5 17.3 %copy-start = (bf16[1,448,576]{2,1,0:T(8,128)(2,1)S(1)}, bf16[1,448,576]{2,1,0:T(8,128)(2,1)}, u32[]{:S(2)}) copy-start(bf16[1,448,576]{2,1,0:T(8,128)(2,1)} %param.8) | copy-start | bytes 1548292
  6.5 80.0 %copy-start.2 = (s32[64]{0:T(128)S(1)}, s32[64]{0:T(128)}, u32[]{:S(2)}) copy-start(s32[64]{0:T(128)} %param.13) | copy-start | bytes 772
  6.5 147.3 %all-gather.2.cloned.1.call-start = ((), (), s32[]{:S(2)}) async-start(), calls=%async_computation.2 | async-start | bytes 5898240 | tf_op jit(solution)/shard_map/all_gather | solution.py:45
  7.6 16.2 %collective-permute-start = (bf16[1,128,448]{2,1,0:T(8,128)(2,1)S(1)}, bf16[1,128,448]{2,1,0:T(8,128)(2,1)S(1)}, u32[]{:S(2)}, u32[]{:S(2)}) collective-permute-start(bf16[1,128,448]{2,1,0:T(8,128)(2,1)S(1)} %copy.29), channel_id=1, source_target_pairs={{0,16},{1,17},{2,18},{3,19},{4,20},{5,21},{6,22},{7,23},{8,24},{9,... | collective-permute-start | bytes 344072 | tf_op jit(solution)/shard_map/ppermute | solution.py:13
  159.7 2.6 %copy-start.3 = (bf16[4096,576]{1,0:T(8,128)(2,1)S(1)}, bf16[4096,576]{1,0:T(8,128)(2,1)}, u32[]{:S(2)}) copy-start(bf16[4096,576]{1,0:T(8,128)(2,1)} %all-gather.2.cloned.1.call-done) | copy-start | bytes 14155780
  162.3 2.8 %copy-start.1 = (bf16[1,4,512,128]{3,2,1,0:T(8,128)(2,1)S(1)}, bf16[1,4,512,128]{3,2,1,0:T(8,128)(2,1)}, u32[]{:S(2)}) copy-start(bf16[1,4,512,128]{3,2,1,0:T(8,128)(2,1)} %param.12) | copy-start | bytes 1572868
Sparse Core Ops, SparseCore 0:
  81.9 71.9 all-gather.1
where the time goes:
time: 173 us
  waiting for transfers between devices  82 us (47%)
  blocking collectives  56.7 us (33%)
  between operations  13.6 us (8%)
  matrix products  10.5 us (6%)
  other arithmetic  4.56 us (3%)
  local copies, waits for them, and re-layouts  4.49 us (3%)
    all_gather x1, waiting for transfers between devices, gathered_by_axis(): array = lax.all_gather(array, axis, axis=dim, tiled=True)  67.1 us
    all_to_all x1, blocking collectives, sent_to_all(): return lax.all_to_all(copies, axis, split_axis=0, concat_axis=0, tiled=True)  23.7 us
    all_to_all x1, blocking collectives, sum_at_owner(): pieces = lax.all_to_all(cut_along(array, dim, size), axis, 0, 0, tiled=True)  21.8 us
    ppermute x1, waiting for transfers between devices, shifted(): return lax.ppermute(array, axis, pairs)  14.9 us
    all_gather x1, blocking collectives, gathered_by_axis(): array = lax.all_gather(array, axis, axis=dim, tiled=True)  11.2 us
    dot_general x1, matrix products, shards(): jnp.dot(query_full, block_rows.T, preferred_element_type=jnp.float32)  5.84 us
  transfers between devices with their start and end apart: 2, of which 2 were waited for; matrix products, arithmetic and copies ran while one was open for 3% of the time, Pallas kernels for 0%

commit v1 on v0

v1 whole, which is shorter than its diff:
```python
import functools

import jax
import jax.numpy as jnp
from jax import lax
from jax.experimental import pallas as pl
from jax.experimental.pallas import tpu as pltpu
from jax.sharding import Mesh
from jax.sharding import PartitionSpec as P

CTX = ("y1", "y0", "x")
SHARE = ("y0", "x")
KEYS = ("y1",)
LANES = 128
LOG2_E = 1.4426950408889634
LOW = -1e30
WHOLE = pl.BlockSpec(memory_space=pltpu.VMEM)
SCALARS = pl.BlockSpec(memory_space=pltpu.SMEM)


def exchange(array, axes):
    return lax.all_to_all(array, axes, 0, 0, tiled=True)


def cost(flops, bytes_accessed):
    return pl.CostEstimate(flops=flops, bytes_accessed=bytes_accessed, transcendentals=0)


def pack_queries(query, copies):
    tokens, heads, width = query.shape
    nope = LANES
    rope = width - nope
    slabs = heads + heads * rope // LANES

    def kernel(query_ref, out_ref):
        rows = query_ref[...]
        for head in range(heads):
            slab = rows[:, head, :nope]
            for copy in range(copies):
                out_ref[copy, head] = slab
        for pair in range(heads // 2):
            slab = jnp.concatenate(
                [rows[:, 2 * pair, nope:], rows[:, 2 * pair + 1, nope:]], axis=-1
            )
            for copy in range(copies):
                out_ref[copy, heads + pair] = slab

    return pl.pallas_call(
        kernel,
        out_shape=jax.ShapeDtypeStruct((copies, slabs, tokens, LANES), query.dtype),
        in_specs=[WHOLE],
        out_specs=WHOLE,
        cost_estimate=cost(0, copies * slabs * tokens * LANES * 2),
        name="pack_queries",
    )(query)


def norm_rows(pieces, gain, copies):
    parts, rows, width = pieces.shape
    latent = gain.shape[-1]

    def kernel(pieces_ref, gain_ref, out_ref):
        raw = pieces_ref[0]
        for part in range(1, parts):
            raw = raw + pieces_ref[part]
        latent_part = raw[:, :latent]
        mean_sq = jnp.mean(latent_part * latent_part, axis=-1, keepdims=True)
        normed = latent_part * lax.rsqrt(mean_sq + 1e-06) * gain_ref[...]
        pad = jnp.zeros((rows, LANES - (width - latent)), jnp.float32)
        row = jnp.concatenate([normed, raw[:, latent:], pad], axis=-1).astype(jnp.bfloat16)
        for copy in range(copies):
            out_ref[copy] = row

    return pl.pallas_call(
        kernel,
        out_shape=jax.ShapeDtypeStruct((copies, rows, latent + LANES), jnp.bfloat16),
        in_specs=[WHOLE, WHOLE],
        out_specs=WHOLE,
        cost_estimate=cost(0, parts * rows * width * 8),
        name="norm_rows",
    )(pieces, gain)


def absorb(block_ids, place, slabs, key_up):
    share, n_slabs, tokens, _ = slabs.shape
    heads, _, latent = key_up.shape
    half = tokens // 2
    n_blocks = block_ids.shape[0]

    def kernel(ids_ref, place_ref, slab_ref, up_ref, out_ref):
        owner = place_ref[0] + pl.program_id(0)
        first = (ids_ref[2 * owner] >= n_blocks // 2).astype(jnp.int32)
        for head in range(heads):
            value = jnp.dot(
                slab_ref[0, head], up_ref[head], preferred_element_type=jnp.float32
            ).astype(jnp.bfloat16)
            rope = slab_ref[0, heads + head // 2]
            if head % 2:
                rope = jnp.concatenate([rope[:, LANES // 2 :], rope[:, : LANES // 2]], axis=-1)
            rows = pl.ds(head * half, half)
            out_ref[0, first, rows, :latent] = value[:half]
            out_ref[0, 1 - first, rows, :latent] = value[half:]
            out_ref[0, first, rows, latent:] = rope[:half]
            out_ref[0, 1 - first, rows, latent:] = rope[half:]

    return pl.pallas_call(
        kernel,
        out_shape=jax.ShapeDtypeStruct(
            (share, 2, heads * half, latent + LANES), jnp.bfloat16
        ),
        grid=(share,),
        in_specs=[
            SCALARS,
            SCALARS,
            pl.BlockSpec((1, n_slabs, tokens, LANES), lambda g: (g, 0, 0, 0)),
            pl.BlockSpec((heads, LANES, latent), lambda g: (0, 0, 0)),
        ],
        out_specs=pl.BlockSpec((1, 2, heads * half, latent + LANES), lambda g: (g, 0, 0, 0)),
        cost_estimate=cost(
            2 * share * heads * tokens * LANES * latent,
            share * heads * tokens * (latent + LANES) * 4,
        ),
        name="absorb",
    )(block_ids, place, slabs, key_up)


def attend(block_ids, place, query_full, keys, value_up, scale):
    share, _, rows, width = query_full.shape
    sources, tokens, _ = keys.shape
    heads, latent, value_dim = value_up.shape
    half = tokens // 2
    n_blocks = block_ids.shape[0]
    n_keys = sources * half
    factor = scale * LOG2_E

    def kernel(ids_ref, place_ref, query_ref, keys_ref, up_ref, out_ref, turned, plain, held, key_pos):
        step = pl.program_id(0)

        @pl.when(step == 0)
        def _():
            spot = lax.broadcasted_iota(jnp.int32, (8, n_keys), 1)
            low_pos = spot
            for source in range(sources):
                owner = place_ref[1] + source * place_ref[2]
                id_first = ids_ref[2 * owner]
                first = (id_first >= n_blocks // 2).astype(jnp.int32)
                low_id = jnp.minimum(id_first, n_blocks - 1 - id_first)
                low_pos = jnp.where(
                    spot // half == source, low_id * half + spot % half, low_pos
                )
                for side in range(2):
                    begin = jnp.where(first == side, 0, half)
                    begin = pl.multiple_of(begin, half)
                    plain[side, pl.ds(source * half, half), :] = keys_ref[
                        source, pl.ds(begin, half), :
                    ]
            key_pos[0] = low_pos
            low_block = low_pos // half
            key_pos[1] = (n_blocks - 1 - low_block) * half + low_pos % half
            for side in range(2):
                turned[side] = plain[side].T

        owner = place_ref[0] + step
        id_first = ids_ref[2 * owner]
        low_id = jnp.minimum(id_first, n_blocks - 1 - id_first)
        within = lax.broadcasted_iota(jnp.int32, (rows, 1), 0) % half

        def score(side, key_side):
            return (
                jnp.dot(query_ref[0, side], turned[key_side], preferred_element_type=jnp.float32)
                * factor
            )

        def masked(side, block):
            seen = key_pos[side, 0:1, :] <= block * half + within
            return seen, jnp.where(seen, score(side, side), LOW)

        lane = lax.broadcasted_iota(jnp.int32, (half, LANES), 1)

        def finish(side, top, total, weighted):
            some = total > 0.0
            safe = jnp.where(some, total, 1.0)
            value = (weighted * (1.0 / safe)).astype(jnp.bfloat16)
            level = jnp.where(some, top + jnp.log2(safe), LOW)
            high = level.astype(jnp.bfloat16).astype(jnp.float32)
            rest = level - high
            middle = rest.astype(jnp.bfloat16).astype(jnp.float32)
            parts = (high, middle, rest - middle)
            tile = jnp.zeros((half, LANES), jnp.float32)
            for head in range(heads):
                span = slice(head * half, (head + 1) * half)
                row = pl.multiple_of(step * tokens + side * half, half)
                held[head, pl.ds(row, half), :] = value[span]
                for at, part in enumerate(parts):
                    tile = jnp.where(lane == 3 * head + at, part[span], tile)
            out_ref[step, pl.ds(side * half, half), heads * value_dim :] = tile.astype(jnp.bfloat16)

        seen, low_low = masked(0, low_id)
        top = jnp.max(low_low, axis=1, keepdims=True)
        expo = jnp.where(seen, jnp.exp2(low_low - top), 0.0)
        total = jnp.sum(expo, axis=1, keepdims=True)
        weighted = jnp.dot(
            expo.astype(jnp.bfloat16), plain[0, :, :latent], preferred_element_type=jnp.float32
        )
        finish(0, top, total, weighted)

        high_low = score(1, 0)
        seen, high_high = masked(1, n_blocks - 1 - low_id)
        top = jnp.maximum(
            jnp.max(high_low, axis=1, keepdims=True), jnp.max(high_high, axis=1, keepdims=True)
        )
        expo_low = jnp.exp2(high_low - top)
        expo_high = jnp.where(seen, jnp.exp2(high_high - top), 0.0)
        total = jnp.sum(expo_low, axis=1, keepdims=True) + jnp.sum(
            expo_high, axis=1, keepdims=True
        )
        weighted = jnp.dot(
            expo_low.astype(jnp.bfloat16), plain[0, :, :latent], preferred_element_type=jnp.float32
        ) + jnp.dot(
            expo_high.astype(jnp.bfloat16), plain[1, :, :latent], preferred_element_type=jnp.float32
        )
        finish(1, top, total, weighted)

        @pl.when(step == share - 1)
        def _():
            for head in range(heads):
                value = jnp.dot(held[head], up_ref[head], preferred_element_type=jnp.float32)
                out_ref[:, :, head * value_dim : (head + 1) * value_dim] = value.astype(
                    jnp.bfloat16
                ).reshape(share, tokens, value_dim)

    out_width = heads * value_dim + LANES
    return pl.pallas_call(
        kernel,
        out_shape=jax.ShapeDtypeStruct((share, tokens, out_width), jnp.bfloat16),
        grid=(share,),
        in_specs=[
            SCALARS,
            SCALARS,
            pl.BlockSpec((1, 2, rows, width), lambda g: (g, 0, 0, 0)),
            pl.BlockSpec((sources, tokens, width), lambda g: (0, 0, 0)),
            pl.BlockSpec((heads, latent, value_dim), lambda g: (0, 0, 0)),
        ],
        out_specs=pl.BlockSpec((share, tokens, out_width), lambda g: (0, 0, 0)),
        scratch_shapes=[
            pltpu.VMEM((2, width, n_keys), jnp.bfloat16),
            pltpu.VMEM((2, n_keys, width), jnp.bfloat16),
            pltpu.VMEM((heads, share * tokens, latent), jnp.bfloat16),
            pltpu.VMEM((2, 8, n_keys), jnp.int32),
        ],
        cost_estimate=cost(
            share * 6 * rows * n_keys * (width + latent), share * rows * width * 4
        ),
        name="attend",
    )(block_ids, place, query_full, keys, value_up)


def combine(block_ids, place, parts, heads):
    share, tokens, width = parts.shape
    value_width = width - LANES
    value_dim = value_width // heads
    half = tokens // 2
    n_blocks = block_ids.shape[0]

    def kernel(ids_ref, place_ref, parts_ref, out_ref):
        first = (ids_ref[2 * place_ref[3]] >= n_blocks // 2).astype(jnp.int32)
        for side in range(2):
            begin = pl.multiple_of(jnp.where(first == side, 0, half), half)
            span = slice(side * half, (side + 1) * half)
            stats = [parts_ref[k, span, value_width:].astype(jnp.float32) for k in range(share)]
            for head in range(heads):
                levels = [
                    s[:, 3 * head : 3 * head + 1]
                    + s[:, 3 * head + 1 : 3 * head + 2]
                    + s[:, 3 * head + 2 : 3 * head + 3]
                    for s in stats
                ]
                top = functools.reduce(jnp.maximum, levels)
                shares = [jnp.exp2(level - top) for level in levels]
                inverse = 1.0 / functools.reduce(jnp.add, shares)
                columns = slice(head * value_dim, (head + 1) * value_dim)
                value = jnp.zeros((half, value_dim), jnp.float32)
                for k in range(share):
                    value += parts_ref[k, span, columns].astype(jnp.float32) * (
                        shares[k] * inverse
                    )
                out_ref[0, pl.ds(begin, half), columns] = value.astype(jnp.bfloat16)

    return pl.pallas_call(
        kernel,
        out_shape=jax.ShapeDtypeStruct((1, tokens, value_width), jnp.bfloat16),
        in_specs=[SCALARS, SCALARS, WHOLE],
        out_specs=WHOLE,
        cost_estimate=cost(0, share * tokens * width * 2),
        name="combine",
    )(block_ids, place, parts)


def shards(outgoing, w_down, kv_gain, queries, w_key_up, w_value_up, block_ids):
    section_idx = lax.axis_index("pp")
    n_y0, n_x, tp_size = (lax.axis_size(a) for a in ("y0", "x", "tp"))
    n_share = n_y0 * n_x
    n_keys = lax.axis_size("y1")
    tokens, heads, query_dim = queries.shape[1:]
    y1, y0, x = (lax.axis_index(a).astype(jnp.int32) for a in CTX)
    column = y0 * n_x + x
    place = jnp.stack([y1 * n_share, column, jnp.int32(n_share), y1 * n_share + column])

    slabs = pack_queries(queries[0], n_share)
    moved = lax.ppermute(outgoing, "pp", [(0, 1)])
    section_in = jnp.where(section_idx == 0, outgoing, moved)[0]
    with jax.named_scope("share"):
        shared = exchange(slabs, SHARE)
    partial_value = jnp.dot(section_in, w_down[0], preferred_element_type=jnp.float32)
    with jax.named_scope("reduce"):
        pieces = exchange(partial_value.reshape(tp_size, tokens // tp_size, -1), ("tp",))
    local = norm_rows(pieces, kv_gain, tp_size)
    with jax.named_scope("spread"):
        key_rows = exchange(local, ("tp",)).reshape(tokens, -1)
    with jax.named_scope("keys"):
        keys = exchange(jnp.broadcast_to(key_rows, (n_keys, *key_rows.shape)), KEYS)

    query_full = absorb(block_ids, place, shared, w_key_up[0])
    part_out = attend(block_ids, place, query_full, keys, w_value_up[0], query_dim**-0.5)
    with jax.named_scope("parts"):
        got = exchange(part_out, SHARE)
    return combine(block_ids, place, got, heads)


def build(torus):
    placed = (
        P("pp", CTX, "tp"),
        P("pp", "tp", None),
        P("pp", None),
        P("pp", CTX, "tp", None),
        P("pp", "tp", None, None),
        P("pp", "tp", None, None),
        P(),
    )
    return jax.shard_map(
        shards, mesh=torus, in_specs=placed, out_specs=P("pp", CTX, "tp"), check_vma=False
    )


def solution(mesh):
    torus = Mesh(
        mesh.devices.reshape(4, 2, 4, mesh.shape["pp"], mesh.shape["tp"]),
        ("y1", "y0", "x", "pp", "tp"),
    )
    return build(torus)
```

time: 173 us -> 156 us (0.902)
  the two profiles are of different devices: /device:TPU:1 before, /device:TPU:64 now
where the time goes in v1:
time: 156 us; the launch traced here: 155 us
  blocking collectives  87.7 us (56%)
  Pallas kernels  28.4 us (18%)
  waiting for transfers between devices  19.1 us (12%)
  starting transfers between devices  14.9 us (10%)
  local copies, waits for them, and re-layouts  3.71 us (2%)
    all_to_all x3, blocking collectives, exchange(): return lax.all_to_all(array, axes, 0, 0, tiled=True)  87.7 us
    all_to_all x2, waiting for transfers between devices, exchange(): return lax.all_to_all(array, axes, 0, 0, tiled=True)  18.2 us
    pallas_call x1, Pallas kernels, attend(): pl.pallas_call(kernel, out_shape=jax.ShapeDtypeStruct((share, tokens, out...  13.4 us
    all_to_all x2, starting transfers between devices, exchange(): return lax.all_to_all(array, axes, 0, 0, tiled=True)  13.2 us
    pallas_call x1, Pallas kernels, absorb(): pl.pallas_call(kernel, out_shape=jax.ShapeDtypeStruct((share, 2, heads *...  7.36 us
    pallas_call x1, Pallas kernels, combine(): pl.pallas_call(kernel, out_shape=jax.ShapeDtypeStruct((1, tokens, value_w...  3.15 us
  transfers between devices with their start and end apart: 3, of which 3 were waited for; matrix products, arithmetic and copies ran while one was open for 1% of the time, Pallas kernels for 7%

profile of v1, /device:TPU:64, one launch (start us, length us, event | category | flops | bytes accessed | tf_op | source)
XLA Modules:
  0.0 154.9 jit_solution(8534496815405062180)
XLA Ops:
  0.0 0.0 copy-start
  0.0 0.0 copy-start.2
  0.0 1.1 copy.12
  1.1 1.7 %collective-permute-start = (bf16[1,128,448]{2,1,0:T(8,128)(2,1)S(1)}, bf16[1,128,448]{2,1,0:T(8,128)(2,1)S(1)}, u32[]{:S(2)}, u32[]{:S(2)}) collective-permute-start(bf16[1,128,448]{2,1,0:T(8,128)(2,1)S(1)} %copy.12), channel_id=1, source_target_pairs={{0,16},{1,17},{2,18},{3,19},{4,20},{5,21},{6,22},{7,23},{8,24},{9,... | collective-permute-start | bytes 344072 | tf_op jit(solution)/shard_map/ppermute | solution.py:310
  2.8 1.0 collective-permute-done
  3.8 0.0 copy-done
  3.8 0.3 fusion
  4.1 38.9 %all_to_all.25.pieces_ref = f32[16,8,576]{2,1,0:T(8,128)} all-to-all(f32[16,8,576]{2,1,0:T(8,128)S(1)} %fusion), channel_id=1, replica_groups=mesh['y1'=4,'y0'=2,'x'=4,'pp'=2,'tp'=16] {'tp'}, dimensions={0} | all-to-all | bytes 589824 | tf_op jit(solution)/shard_map/reduce/all_to_all | solution.py:22
  42.9 1.7 %norm_rows.1 = bf16[16,8,640]{2,1,0:T(8,128)(2,1)} custom-call(f32[16,8,576]{2,1,0:T(8,128)} %all_to_all.25.pieces_ref, f32[1,512]{1,0:T(1,128)} %gain_ref.1), custom_call_target="tpu_custom_call" | custom-call | bytes 589824 | tf_op jit(solution)/shard_map/norm_rows/pallas_call | solution.py:74
  44.7 7.0 %all-to-all-start.2 = ((bf16[16,8,640]{2,1,0:T(8,128)(2,1)}), bf16[16,8,640]{2,1,0:T(8,128)(2,1)S(1)}, u32[]{:S(2)}, u32[]{:S(2)}) async-start(bf16[16,8,640]{2,1,0:T(8,128)(2,1)} %norm_rows.1), calls=%async_computation.2 | async-start | bytes 327680 | tf_op jit(solution)/shard_map/spread/all_to_all | solution.py:22
  51.6 0.0 copy-done.2
  51.7 0.9 copy.10
  52.5 2.8 %pack_queries.1 = bf16[8,6,128,128]{3,2,1,0:T(8,128)(2,1)} custom-call(bf16[128,4,192]{2,1,0:T(4,128)(2,1)} %bitcast.14), custom_call_target="tpu_custom_call" | custom-call | bytes 1572864 | tf_op jit(solution)/shard_map/pack_queries/pallas_call | solution.py:48
  55.3 11.3 %all-to-all-done.2 = bf16[16,8,640]{2,1,0:T(8,128)(2,1)S(1)} async-done(((bf16[16,8,640]{2,1,0:T(8,128)(2,1)}), bf16[16,8,640]{2,1,0:T(8,128)(2,1)S(1)}, u32[]{:S(2)}, u32[]{:S(2)}) %all-to-all-start.2) | async-done | bytes 163872 | tf_op jit(solution)/shard_map/spread/all_to_all | solution.py:22
  66.6 25.8 %all_to_all.26.slab_ref = bf16[8,6,128,128]{3,2,1,0:T(8,128)(2,1)} all-to-all(bf16[8,6,128,128]{3,2,1,0:T(8,128)(2,1)} %pack_queries.1), channel_id=1, replica_groups=mesh['y1'=4,'y0'=2,'x'=4,'pp'=2,'tp'=16] {'y0','x'}, dimensions={0} | all-to-all | bytes 3145728 | tf_op jit(solution)/shard_map/share/all_to_all | solution.py:22
  92.4 0.9 broadcast_in_dim.3
  93.3 6.2 %all-to-all-start.3 = ((bf16[4,128,640]{2,1,0:T(8,128)(2,1)}), bf16[4,128,640]{2,1,0:T(8,128)(2,1)S(1)}, u32[]{:S(2)}, u32[]{:S(2)}) async-start(bf16[4,128,640]{2,1,0:T(8,128)(2,1)} %broadcast_in_dim.3), calls=%async_computation.3 | async-start | bytes 1310720 | tf_op jit(solution)/shard_map/keys/all_to_all | solution.py:22
  99.5 0.7 pad_add_fusion.place_ref
  100.2 7.4 %absorb.1.query_ref = bf16[8,2,256,640]{3,2,1,0:T(8,128)(2,1)} custom-call(s32[64]{0:T(128)} %ids_ref.5, s32[4]{0:T(128)} %pad_add_fusion.place_ref, bf16[8,6,128,128]{3,2,1,0:T(8,128)(2,1)} %all_to_all.26.slab_ref, bf16[4,128,512]{2,1,0:T(8,128)(2,1)} %bitcast.16), custom_call_target="tpu_custom_call" | custom-call | flops 536870912 | bytes 10485760 | tf_op jit(solution)/shard_map/absorb/pallas_call | solution.py:106
  107.6 6.9 %all-to-all-done.3.keys_ref = bf16[4,128,640]{2,1,0:T(8,128)(2,1)S(1)} async-done(((bf16[4,128,640]{2,1,0:T(8,128)(2,1)}), bf16[4,128,640]{2,1,0:T(8,128)(2,1)S(1)}, u32[]{:S(2)}, u32[]{:S(2)}) %all-to-all-start.3) | async-done | bytes 655392 | tf_op jit(solution)/shard_map/keys/all_to_all | solution.py:22
  114.4 0.0 copy-start.1
  114.5 0.9 copy-done.1
  115.3 13.4 %attend.1 = bf16[8,128,640]{2,1,0:T(8,128)(2,1)} custom-call(s32[64]{0:T(128)} %ids_ref.5, s32[4]{0:T(128)} %pad_add_fusion.place_ref, bf16[8,2,256,640]{3,2,1,0:T(8,128)(2,1)} %absorb.1.query_ref, bf16[4,128,640]{2,1,0:T(8,128)(2,1)} %copy-done.1, bf16[4,512,128]{2,1,0:T(8,128)(2,1)} %bitcast.17), custom_call_target="tpu_custom_call" | custom-call | flops 3623878656 | bytes 5242880 | tf_op jit(solution)/shard_map/attend/pallas_call | solution.py:233
  128.7 23.1 %all_to_all.27.parts_ref = bf16[8,128,640]{2,1,0:T(8,128)(2,1)} all-to-all(bf16[8,128,640]{2,1,0:T(8,128)(2,1)} %attend.1), channel_id=1, replica_groups=mesh['y1'=4,'y0'=2,'x'=4,'pp'=2,'tp'=16] {'y0','x'}, dimensions={0} | all-to-all | bytes 2621440 | tf_op jit(solution)/shard_map/parts/all_to_all | solution.py:22
  151.8 3.1 %combine.1 = bf16[1,128,512]{2,1,0:T(8,128)(2,1)} custom-call(s32[64]{0:T(128)} %ids_ref.5, s32[4]{0:T(128)} %pad_add_fusion.place_ref, bf16[8,128,640]{2,1,0:T(8,128)(2,1)} %all_to_all.27.parts_ref), custom_call_target="tpu_custom_call" | custom-call | bytes 1310720 | tf_op jit(solution)/shard_map/combine/pallas_call | solution.py:289
Async XLA Ops:
  0.0 3.8 %copy-start = (bf16[1,448,576]{2,1,0:T(8,128)(2,1)S(1)}, bf16[1,448,576]{2,1,0:T(8,128)(2,1)}, u32[]{:S(2)}) copy-start(bf16[1,448,576]{2,1,0:T(8,128)(2,1)} %param.8) | copy-start | bytes 1548292
  0.0 51.6 %copy-start.2 = (bf16[1,128,4,192]{1,3,2,0:T(8,128)(2,1)S(1)}, bf16[1,128,4,192]{1,3,2,0:T(8,128)(2,1)}, u32[]{:S(2)}) copy-start(bf16[1,128,4,192]{1,3,2,0:T(8,128)(2,1)} %param.10) | copy-start | bytes 589828
  1.1 2.7 %collective-permute-start = (bf16[1,128,448]{2,1,0:T(8,128)(2,1)S(1)}, bf16[1,128,448]{2,1,0:T(8,128)(2,1)S(1)}, u32[]{:S(2)}, u32[]{:S(2)}) collective-permute-start(bf16[1,128,448]{2,1,0:T(8,128)(2,1)S(1)} %copy.12), channel_id=1, source_target_pairs={{0,16},{1,17},{2,18},{3,19},{4,20},{5,21},{6,22},{7,23},{8,24},{9,... | collective-permute-start | bytes 344072 | tf_op jit(solution)/shard_map/ppermute | solution.py:310
  44.7 22.0 %all-to-all-start.2 = ((bf16[16,8,640]{2,1,0:T(8,128)(2,1)}), bf16[16,8,640]{2,1,0:T(8,128)(2,1)S(1)}, u32[]{:S(2)}, u32[]{:S(2)}) async-start(bf16[16,8,640]{2,1,0:T(8,128)(2,1)} %norm_rows.1), calls=%async_computation.2 | async-start | bytes 327680 | tf_op jit(solution)/shard_map/spread/all_to_all | solution.py:22
  93.3 21.1 %all-to-all-start.3 = ((bf16[4,128,640]{2,1,0:T(8,128)(2,1)}), bf16[4,128,640]{2,1,0:T(8,128)(2,1)S(1)}, u32[]{:S(2)}, u32[]{:S(2)}) async-start(bf16[4,128,640]{2,1,0:T(8,128)(2,1)} %broadcast_in_dim.3), calls=%async_computation.3 | async-start | bytes 1310720 | tf_op jit(solution)/shard_map/keys/all_to_all | solution.py:22
  114.4 0.9 copy-start.1

commit v2 on v1

--- a/solution.py
+++ b/solution.py
@@ -8,9 +8,9 @@
 from jax.sharding import Mesh
 from jax.sharding import PartitionSpec as P
 
-CTX = ("y1", "y0", "x")
-SHARE = ("y0", "x")
-KEYS = ("y1",)
+CTX = ("y", "x")
+SHARE = "x"
+KEYS = "y"
 LANES = 128
 LOG2_E = 1.4426950408889634
 LOW = -1e30
@@ -26,7 +26,7 @@
     return pl.CostEstimate(flops=flops, bytes_accessed=bytes_accessed, transcendentals=0)
 
 
-def pack_queries(query, copies):
+def pack_queries(query):
     tokens, heads, width = query.shape
     nope = LANES
     rope = width - nope
@@ -35,24 +35,41 @@
     def kernel(query_ref, out_ref):
         rows = query_ref[...]
         for head in range(heads):
-            slab = rows[:, head, :nope]
-            for copy in range(copies):
-                out_ref[copy, head] = slab
+            out_ref[head] = rows[:, head, :nope]
         for pair in range(heads // 2):
-            slab = jnp.concatenate(
+            out_ref[heads + pair] = jnp.concatenate(
                 [rows[:, 2 * pair, nope:], rows[:, 2 * pair + 1, nope:]], axis=-1
             )
-            for copy in range(copies):
-                out_ref[copy, heads + pair] = slab
-
-    return pl.pallas_call(
-        kernel,
-        out_shape=jax.ShapeDtypeStruct((copies, slabs, tokens, LANES), query.dtype),
+
+    return pl.pallas_call(
+        kernel,
+        out_shape=jax.ShapeDtypeStruct((slabs, tokens, LANES), query.dtype),
         in_specs=[WHOLE],
         out_specs=WHOLE,
-        cost_estimate=cost(0, copies * slabs * tokens * LANES * 2),
+        cost_estimate=cost(0, 2 * slabs * tokens * LANES * 2),
         name="pack_queries",
     )(query)
+
+
+def project(section_in, w_down, pieces):
+    tokens, depth = section_in.shape
+    width = w_down.shape[-1]
+    padded = -(-width // LANES) * LANES
+    rows = tokens // pieces
+
+    def kernel(in_ref, down_ref, out_ref):
+        value = jnp.dot(in_ref[...], down_ref[...], preferred_element_type=jnp.float32)
+        out_ref[:, :, :width] = value.reshape(pieces, rows, width)
+        out_ref[:, :, width:] = jnp.zeros((pieces, rows, padded - width), jnp.float32)
+
+    return pl.pallas_call(
+        kernel,
+        out_shape=jax.ShapeDtypeStruct((pieces, rows, padded), jnp.float32),
+        in_specs=[WHOLE, WHOLE],
+        out_specs=WHOLE,
+        cost_estimate=cost(2 * tokens * depth * width, tokens * padded * 4),
+        name="project",
+    )(section_in, w_down)
 
 
 def norm_rows(pieces, gain, copies):
@@ -66,8 +83,7 @@
         latent_part = raw[:, :latent]
         mean_sq = jnp.mean(latent_part * latent_part, axis=-1, keepdims=True)
         normed = latent_part * lax.rsqrt(mean_sq + 1e-06) * gain_ref[...]
-        pad = jnp.zeros((rows, LANES - (width - latent)), jnp.float32)
-        row = jnp.concatenate([normed, raw[:, latent:], pad], axis=-1).astype(jnp.bfloat16)
+        row = jnp.concatenate([normed, raw[:, latent:]], axis=-1).astype(jnp.bfloat16)
         for copy in range(copies):
             out_ref[copy] = row
 
@@ -82,46 +98,45 @@
 
 
 def absorb(block_ids, place, slabs, key_up):
-    share, n_slabs, tokens, _ = slabs.shape
+    share = len(slabs)
+    _, tokens, _ = slabs[0].shape
     heads, _, latent = key_up.shape
     half = tokens // 2
     n_blocks = block_ids.shape[0]
 
-    def kernel(ids_ref, place_ref, slab_ref, up_ref, out_ref):
-        owner = place_ref[0] + pl.program_id(0)
-        first = (ids_ref[2 * owner] >= n_blocks // 2).astype(jnp.int32)
-        for head in range(heads):
-            value = jnp.dot(
-                slab_ref[0, head], up_ref[head], preferred_element_type=jnp.float32
-            ).astype(jnp.bfloat16)
-            rope = slab_ref[0, heads + head // 2]
-            if head % 2:
-                rope = jnp.concatenate([rope[:, LANES // 2 :], rope[:, : LANES // 2]], axis=-1)
-            rows = pl.ds(head * half, half)
-            out_ref[0, first, rows, :latent] = value[:half]
-            out_ref[0, 1 - first, rows, :latent] = value[half:]
-            out_ref[0, first, rows, latent:] = rope[:half]
-            out_ref[0, 1 - first, rows, latent:] = rope[half:]
+    def kernel(ids_ref, place_ref, *refs):
+        slab_refs, up_ref, out_ref = refs[:share], refs[share], refs[share + 1]
+        for back, slab_ref in enumerate(slab_refs):
+            owner = place_ref[0] + lax.rem(place_ref[1] + share - back, share)
+            first = (ids_ref[2 * owner] >= n_blocks // 2).astype(jnp.int32)
+            for head in range(heads):
+                value = jnp.dot(
+                    slab_ref[head], up_ref[head], preferred_element_type=jnp.float32
+                ).astype(jnp.bfloat16)
+                rope = slab_ref[heads + head // 2]
+                if head % 2:
+                    rope = jnp.concatenate(
+                        [rope[:, LANES // 2 :], rope[:, : LANES // 2]], axis=-1
+                    )
+                rows = pl.ds(head * half, half)
+                out_ref[back, first, rows, :latent] = value[:half]
+                out_ref[back, 1 - first, rows, :latent] = value[half:]
+                out_ref[back, first, rows, latent:] = rope[:half]
+                out_ref[back, 1 - first, rows, latent:] = rope[half:]
 
     return pl.pallas_call(
         kernel,
         out_shape=jax.ShapeDtypeStruct(
             (share, 2, heads * half, latent + LANES), jnp.bfloat16
         ),
-        grid=(share,),
-        in_specs=[
-            SCALARS,
-            SCALARS,
-            pl.BlockSpec((1, n_slabs, tokens, LANES), lambda g: (g, 0, 0, 0)),
-            pl.BlockSpec((heads, LANES, latent), lambda g: (0, 0, 0)),
-        ],
-        out_specs=pl.BlockSpec((1, 2, heads * half, latent + LANES), lambda g: (g, 0, 0, 0)),
+        in_specs=[SCALARS, SCALARS] + [WHOLE] * (share + 1),
+        out_specs=WHOLE,
         cost_estimate=cost(
             2 * share * heads * tokens * LANES * latent,
             share * heads * tokens * (latent + LANES) * 4,
         ),
         name="absorb",
-    )(block_ids, place, slabs, key_up)
+    )(block_ids, place, *slabs, key_up)
 
 
 def attend(block_ids, place, query_full, keys, value_up, scale):
@@ -160,8 +175,8 @@
             for side in range(2):
                 turned[side] = plain[side].T
 
-        owner = place_ref[0] + step
-        id_first = ids_ref[2 * owner]
+        receiver = lax.rem(place_ref[1] + share - step, share)
+        id_first = ids_ref[2 * (place_ref[0] + receiver)]
         low_id = jnp.minimum(id_first, n_blocks - 1 - id_first)
         within = lax.broadcasted_iota(jnp.int32, (rows, 1), 0) % half
 
@@ -189,11 +204,11 @@
             tile = jnp.zeros((half, LANES), jnp.float32)
             for head in range(heads):
                 span = slice(head * half, (head + 1) * half)
-                row = pl.multiple_of(step * tokens + side * half, half)
+                row = pl.multiple_of(receiver * tokens + side * half, half)
                 held[head, pl.ds(row, half), :] = value[span]
                 for at, part in enumerate(parts):
                     tile = jnp.where(lane == 3 * head + at, part[span], tile)
-            out_ref[step, pl.ds(side * half, half), heads * value_dim :] = tile.astype(jnp.bfloat16)
+            out_ref[receiver, pl.ds(side * half, half), heads * value_dim :] = tile.astype(jnp.bfloat16)
 
         seen, low_low = masked(0, low_id)
         top = jnp.max(low_low, axis=1, keepdims=True)
@@ -263,7 +278,7 @@
     n_blocks = block_ids.shape[0]
 
     def kernel(ids_ref, place_ref, parts_ref, out_ref):
-        first = (ids_ref[2 * place_ref[3]] >= n_blocks // 2).astype(jnp.int32)
+        first = (ids_ref[2 * (place_ref[0] + place_ref[1])] >= n_blocks // 2).astype(jnp.int32)
         for side in range(2):
             begin = pl.multiple_of(jnp.where(first == side, 0, half), half)
             span = slice(side * half, (side + 1) * half)
@@ -298,32 +313,25 @@
 
 def shards(outgoing, w_down, kv_gain, queries, w_key_up, w_value_up, block_ids):
     section_idx = lax.axis_index("pp")
-    n_y0, n_x, tp_size = (lax.axis_size(a) for a in ("y0", "x", "tp"))
-    n_share = n_y0 * n_x
-    n_keys = lax.axis_size("y1")
+    n_share, n_keys, tp_size = (lax.axis_size(a) for a in (SHARE, KEYS, "tp"))
     tokens, heads, query_dim = queries.shape[1:]
-    y1, y0, x = (lax.axis_index(a).astype(jnp.int32) for a in CTX)
-    column = y0 * n_x + x
-    place = jnp.stack([y1 * n_share, column, jnp.int32(n_share), y1 * n_share + column])
-
-    slabs = pack_queries(queries[0], n_share)
+    y, x = (lax.axis_index(a).astype(jnp.int32) for a in CTX)
+    place = jnp.stack([y * n_share, x, jnp.int32(n_share)])
+
     moved = lax.ppermute(outgoing, "pp", [(0, 1)])
     section_in = jnp.where(section_idx == 0, outgoing, moved)[0]
-    with jax.named_scope("share"):
-        shared = exchange(slabs, SHARE)
-    partial_value = jnp.dot(section_in, w_down[0], preferred_element_type=jnp.float32)
-    with jax.named_scope("reduce"):
-        pieces = exchange(partial_value.reshape(tp_size, tokens // tp_size, -1), ("tp",))
+    partial_value = project(section_in, w_down[0], tp_size)
+    pieces = exchange(partial_value, ("tp",))
+    slabs = [pack_queries(queries[0])]
+    for ahead in range(1, n_share):
+        pairs = [(i, (i + ahead) % n_share) for i in range(n_share)]
+        slabs.append(lax.ppermute(slabs[0], SHARE, pairs))
     local = norm_rows(pieces, kv_gain, tp_size)
-    with jax.named_scope("spread"):
-        key_rows = exchange(local, ("tp",)).reshape(tokens, -1)
-    with jax.named_scope("keys"):
-        keys = exchange(jnp.broadcast_to(key_rows, (n_keys, *key_rows.shape)), KEYS)
-
-    query_full = absorb(block_ids, place, shared, w_key_up[0])
+    key_rows = exchange(local, ("tp",)).reshape(tokens, -1)
+    query_full = absorb(block_ids, place, slabs, w_key_up[0])
+    keys = exchange(jnp.broadcast_to(key_rows, (n_keys, *key_rows.shape)), (KEYS,))
     part_out = attend(block_ids, place, query_full, keys, w_value_up[0], query_dim**-0.5)
-    with jax.named_scope("parts"):
-        got = exchange(part_out, SHARE)
+    got = exchange(part_out, (SHARE,))
     return combine(block_ids, place, got, heads)
 
 
@@ -344,7 +352,7 @@
 
 def solution(mesh):
     torus = Mesh(
-        mesh.devices.reshape(4, 2, 4, mesh.shape["pp"], mesh.shape["tp"]),
-        ("y1", "y0", "x", "pp", "tp"),
+        mesh.devices.reshape(8, 4, mesh.shape["pp"], mesh.shape["tp"]),
+        ("y", "x", "pp", "tp"),
     )
     return build(torus)

time: 156 us -> 142 us (0.910)
  blocking collectives: 87.7 us -> 76.6 us
  Pallas kernels: 28.4 us -> 22.7 us
  starting transfers between devices: 14.9 us -> 19.2 us
  waiting for transfers between devices: 19.1 us -> 16.3 us
    all_to_all x3, blocking collectives: 87.7 us -> 76.6 us  [exchange(): return lax.all_to_all(array, axes, 0, 0, tiled=True)]
    ppermute x0 -> x3, starting transfers between devices: none -> 10.2 us  [shards(): slabs.append(lax.ppermute(slabs[0], SHARE, pairs))]
    all_to_all x2 -> x1, waiting for transfers between devices: 18.2 us -> 8.48 us  [exchange(): return lax.all_to_all(array, axes, 0, 0, tiled=True)]
    ppermute x0 -> x3, waiting for transfers between devices: none -> 6.83 us  [shards(): slabs.append(lax.ppermute(slabs[0], SHARE, pairs))]
    all_to_all x2 -> x1, starting transfers between devices: 13.2 us -> 7.24 us  [exchange(): return lax.all_to_all(array, axes, 0, 0, tiled=True)]
    pallas_call x1, Pallas kernels: 7.36 us -> 3.63 us  [absorb(): pl.pallas_call(kernel, out_shape=jax.ShapeDtypeStruct((share, 2, heads *...]
    pallas_call x1, Pallas kernels: 13.4 us -> 10.7 us  [attend(): pl.pallas_call(kernel, out_shape=jax.ShapeDtypeStruct((share, tokens, out...]
    pallas_call x1 -> x2, Pallas kernels: 2.83 us -> 4.21 us  [the longest x1 2.13 us: project(): pl.pallas_call(kernel, out_shape=jax.ShapeDtypeStruct((pieces, rows, padd...]
  transfers between devices with their start and end apart: 3 -> 5, of which waited for: 3 -> 5; matrix products, arithmetic and copies ran while one was open for 1% -> 1% of each run, Pallas kernels for 7% -> 4%
where the time goes in v2:
time: 142 us; the launch traced here: 141 us
  blocking collectives  76.6 us (54%)
  Pallas kernels  22.7 us (16%)
  starting transfers between devices  19.2 us (14%)
  waiting for transfers between devices  16.3 us (11%)
  local copies, waits for them, and re-layouts  4.79 us (3%)
    all_to_all x3, blocking collectives, exchange(): return lax.all_to_all(array, axes, 0, 0, tiled=True)  76.6 us
    pallas_call x1, Pallas kernels, attend(): pl.pallas_call(kernel, out_shape=jax.ShapeDtypeStruct((share, tokens, out...  10.7 us
    ppermute x3, starting transfers between devices, shards(): slabs.append(lax.ppermute(slabs[0], SHARE, pairs))  10.2 us
    all_to_all x1, waiting for transfers between devices, exchange(): return lax.all_to_all(array, axes, 0, 0, tiled=True)  8.48 us
    all_to_all x1, starting transfers between devices, exchange(): return lax.all_to_all(array, axes, 0, 0, tiled=True)  7.24 us
    ppermute x3, waiting for transfers between devices, shards(): slabs.append(lax.ppermute(slabs[0], SHARE, pairs))  6.83 us
    pallas_call x1, Pallas kernels, absorb(): pl.pallas_call(kernel, out_shape=jax.ShapeDtypeStruct((share, 2, heads *...  3.63 us
    unnamed x12, local copies, waits for them, and re-layouts  3.62 us
  transfers between devices with their start and end apart: 5, of which 5 were waited for; matrix products, arithmetic and copies ran while one was open for 1% of the time, Pallas kernels for 4%

profile of v2, /device:TPU:64, one launch (start us, length us, event | category | flops | bytes accessed | tf_op | source)
XLA Modules:
  0.0 140.9 jit_solution(12808553114181096124)
XLA Ops:
  0.0 1.0 copy.10
  1.0 1.7 %collective-permute-start.3 = (bf16[1,128,448]{2,1,0:T(8,128)(2,1)S(1)}, bf16[1,128,448]{2,1,0:T(8,128)(2,1)S(1)}, u32[]{:S(2)}, u32[]{:S(2)}) collective-permute-start(bf16[1,128,448]{2,1,0:T(8,128)(2,1)S(1)} %copy.10), channel_id=1, source_target_pairs={{0,16},{1,17},{2,18},{3,19},{4,20},{5,21},{6,22},{7,23},{8,24},{9,... | collective-permute-start | bytes 344072 | tf_op jit(solution)/shard_map/ppermute | solution.py:321
  2.8 1.0 collective-permute-done.3
  3.7 0.7 select_bitcast_fusion.in_ref
  4.4 2.1 %project.1 = f32[16,8,640]{2,1,0:T(8,128)} custom-call(bf16[128,448]{1,0:T(8,128)(2,1)} %select_bitcast_fusion.in_ref, bf16[448,576]{1,0:T(8,128)(2,1)} %bitcast.11), custom_call_target="tpu_custom_call" | custom-call | flops 66060288 | bytes 327680 | tf_op jit(solution)/shard_map/project/pallas_call | solution.py:65
  6.5 39.1 %all_to_all.20.pieces_ref = f32[16,8,640]{2,1,0:T(8,128)} all-to-all(f32[16,8,640]{2,1,0:T(8,128)} %project.1), channel_id=1, replica_groups=mesh['y'=8,'x'=4,'pp'=2,'tp'=16] {'tp'}, dimensions={0} | all-to-all | bytes 655360 | tf_op jit(solution)/shard_map/all_to_all | solution.py:22
  45.6 1.8 %norm_rows.1 = bf16[16,8,640]{2,1,0:T(8,128)(2,1)} custom-call(f32[16,8,640]{2,1,0:T(8,128)} %all_to_all.20.pieces_ref, f32[1,512]{1,0:T(1,128)} %gain_ref.1), custom_call_target="tpu_custom_call" | custom-call | bytes 655360 | tf_op jit(solution)/shard_map/norm_rows/pallas_call | solution.py:90
  47.3 22.0 %all_to_all.21 = bf16[16,8,640]{2,1,0:T(8,128)(2,1)S(1)} all-to-all(bf16[16,8,640]{2,1,0:T(8,128)(2,1)} %norm_rows.1), channel_id=1, replica_groups=mesh['y'=8,'x'=4,'pp'=2,'tp'=16] {'tp'}, dimensions={0} | all-to-all | bytes 327680 | tf_op jit(solution)/shard_map/all_to_all | solution.py:22
  69.3 1.2 broadcast_in_dim.3
  70.5 0.0 copy-start.4
  70.5 7.2 %all-to-all-start.2 = ((bf16[8,128,640]{2,1,0:T(8,128)(2,1)}), bf16[8,128,640]{2,1,0:T(8,128)(2,1)S(1)}, u32[]{:S(2)}, u32[]{:S(2)}) async-start(bf16[8,128,640]{2,1,0:T(8,128)(2,1)} %broadcast_in_dim.3), calls=%async_computation.2 | async-start | bytes 2621440 | tf_op jit(solution)/shard_map/all_to_all | solution.py:22
  77.7 0.0 copy-done.4
  77.7 0.9 copy.8
  78.6 2.1 %pack_queries.1.refs_0_ = bf16[6,128,128]{2,1,0:T(8,128)(2,1)} custom-call(bf16[128,4,192]{2,1,0:T(4,128)(2,1)} %bitcast.9), custom_call_target="tpu_custom_call" | custom-call | bytes 393216 | tf_op jit(solution)/shard_map/pack_queries/pallas_call | solution.py:44
  80.7 4.6 %collective-permute-start.2 = (bf16[6,128,128]{2,1,0:T(8,128)(2,1)}, bf16[6,128,128]{2,1,0:T(8,128)(2,1)S(1)}, u32[]{:S(2)}, u32[]{:S(2)}) collective-permute-start(bf16[6,128,128]{2,1,0:T(8,128)(2,1)} %pack_queries.1.refs_0_), channel_id=1, source_target_pairs={{0,96},{32,0},{64,32},{96,64},{1,97},{33,1},{65,33},{97,65},{2,98}... | collective-permute-start | bytes 589832 | tf_op jit(solution)/shard_map/ppermute | solution.py:328
  85.3 2.7 %collective-permute-start.1 = (bf16[6,128,128]{2,1,0:T(8,128)(2,1)}, bf16[6,128,128]{2,1,0:T(8,128)(2,1)S(1)}, u32[]{:S(2)}, u32[]{:S(2)}) collective-permute-start(bf16[6,128,128]{2,1,0:T(8,128)(2,1)} %pack_queries.1.refs_0_), channel_id=1, source_target_pairs={{0,64},{32,96},{64,0},{96,32},{1,65},{33,97},{65,1},{97,33},{2,66}... | collective-permute-start | bytes 589832 | tf_op jit(solution)/shard_map/ppermute | solution.py:328
  88.0 2.8 %collective-permute-start = (bf16[6,128,128]{2,1,0:T(8,128)(2,1)}, bf16[6,128,128]{2,1,0:T(8,128)(2,1)S(1)}, u32[]{:S(2)}, u32[]{:S(2)}) collective-permute-start(bf16[6,128,128]{2,1,0:T(8,128)(2,1)} %pack_queries.1.refs_0_), channel_id=1, source_target_pairs={{0,32},{32,64},{64,96},{96,0},{1,33},{33,65},{65,97},{97,1},{2,34}... | collective-permute-start | bytes 589832 | tf_op jit(solution)/shard_map/ppermute | solution.py:328
  90.9 0.6 pad_add_fusion.place_ref
  91.5 1.5 %collective-permute-done.2.refs_3_ = bf16[6,128,128]{2,1,0:T(8,128)(2,1)S(1)} collective-permute-done((bf16[6,128,128]{2,1,0:T(8,128)(2,1)}, bf16[6,128,128]{2,1,0:T(8,128)(2,1)S(1)}, u32[]{:S(2)}, u32[]{:S(2)}) %collective-permute-start.2) | collective-permute-done | bytes 196640 | tf_op jit(solution)/shard_map/ppermute | solution.py:328
  93.1 0.0 copy-start.1
  93.1 3.3 %collective-permute-done.1.refs_2_ = bf16[6,128,128]{2,1,0:T(8,128)(2,1)S(1)} collective-permute-done((bf16[6,128,128]{2,1,0:T(8,128)(2,1)}, bf16[6,128,128]{2,1,0:T(8,128)(2,1)S(1)}, u32[]{:S(2)}, u32[]{:S(2)}) %collective-permute-start.1) | collective-permute-done | bytes 196640 | tf_op jit(solution)/shard_map/ppermute | solution.py:328
  96.3 0.0 copy-start.2
  96.3 2.0 %collective-permute-done.refs_1_ = bf16[6,128,128]{2,1,0:T(8,128)(2,1)S(1)} collective-permute-done((bf16[6,128,128]{2,1,0:T(8,128)(2,1)}, bf16[6,128,128]{2,1,0:T(8,128)(2,1)S(1)}, u32[]{:S(2)}, u32[]{:S(2)}) %collective-permute-start) | collective-permute-done | bytes 196640 | tf_op jit(solution)/shard_map/ppermute | solution.py:328
  98.4 0.0 copy-done.1
  98.4 0.0 copy-done.2
  98.4 0.7 copy-done.3
  99.0 3.6 %absorb.1.query_ref = bf16[4,2,256,640]{3,2,1,0:T(8,128)(2,1)} custom-call(s32[64]{0:T(128)} %ids_ref.5, s32[3]{0:T(128)} %pad_add_fusion.place_ref, bf16[6,128,128]{2,1,0:T(8,128)(2,1)} %pack_queries.1.refs_0_, bf16[6,128,128]{2,1,0:T(8,128)(2,1)} %copy-done.3, bf16[6,128,128]{2,1,0:T(8,128)(2,1)} %copy-done.2, bf16[6,128,128]{2,1,0:T(8,128)(2,1)} %copy-done.1, ...), custom_call_target="tpu_custom_call" | custom-call | flops 268435456 | bytes 5242880 | tf_op jit(solution)/shard_map/absorb/pallas_call | solution.py:127
  102.7 8.5 %all-to-all-done.2.keys_ref = bf16[8,128,640]{2,1,0:T(8,128)(2,1)S(1)} async-done(((bf16[8,128,640]{2,1,0:T(8,128)(2,1)}), bf16[8,128,640]{2,1,0:T(8,128)(2,1)S(1)}, u32[]{:S(2)}, u32[]{:S(2)}) %all-to-all-start.2) | async-done | bytes 1310752 | tf_op jit(solution)/shard_map/all_to_all | solution.py:22
  111.1 1.1 copy-done
  112.2 10.7 %attend.1 = bf16[4,128,640]{2,1,0:T(8,128)(2,1)} custom-call(s32[64]{0:T(128)} %ids_ref.5, s32[3]{0:T(128)} %pad_add_fusion.place_ref, bf16[4,2,256,640]{3,2,1,0:T(8,128)(2,1)} %absorb.1.query_ref, bf16[8,128,640]{2,1,0:T(8,128)(2,1)} %copy-done, bf16[4,512,128]{2,1,0:T(8,128)(2,1)} %bitcast.13), custom_call_target="tpu_custom_call" | custom-call | flops 3623878656 | bytes 2621440 | tf_op jit(solution)/shard_map/attend/pallas_call | solution.py:248
  122.9 15.6 %all_to_all.22.parts_ref = bf16[4,128,640]{2,1,0:T(8,128)(2,1)} all-to-all(bf16[4,128,640]{2,1,0:T(8,128)(2,1)} %attend.1), channel_id=1, replica_groups=mesh['y'=8,'x'=4,'pp'=2,'tp'=16] {'x'}, dimensions={0} | all-to-all | bytes 1310720 | tf_op jit(solution)/shard_map/all_to_all | solution.py:22
  138.4 2.4 %combine.1 = bf16[1,128,512]{2,1,0:T(8,128)(2,1)} custom-call(s32[64]{0:T(128)} %ids_ref.5, s32[3]{0:T(128)} %pad_add_fusion.place_ref, bf16[4,128,640]{2,1,0:T(8,128)(2,1)} %all_to_all.22.parts_ref), custom_call_target="tpu_custom_call" | custom-call | bytes 655360 | tf_op jit(solution)/shard_map/combine/pallas_call | solution.py:304
  (2 shorter events, 0.0 us)
Async XLA Ops:
  1.0 2.7 %collective-permute-start.3 = (bf16[1,128,448]{2,1,0:T(8,128)(2,1)S(1)}, bf16[1,128,448]{2,1,0:T(8,128)(2,1)S(1)}, u32[]{:S(2)}, u32[]{:S(2)}) collective-permute-start(bf16[1,128,448]{2,1,0:T(8,128)(2,1)S(1)} %copy.10), channel_id=1, source_target_pairs={{0,16},{1,17},{2,18},{3,19},{4,20},{5,21},{6,22},{7,23},{8,24},{9,... | collective-permute-start | bytes 344072 | tf_op jit(solution)/shard_map/ppermute | solution.py:321
  70.5 7.2 %copy-start.4 = (bf16[1,128,4,192]{1,3,2,0:T(8,128)(2,1)S(1)}, bf16[1,128,4,192]{1,3,2,0:T(8,128)(2,1)}, u32[]{:S(2)}) copy-start(bf16[1,128,4,192]{1,3,2,0:T(8,128)(2,1)} %param.10) | copy-start | bytes 589828
  70.5 40.7 %all-to-all-start.2 = ((bf16[8,128,640]{2,1,0:T(8,128)(2,1)}), bf16[8,128,640]{2,1,0:T(8,128)(2,1)S(1)}, u32[]{:S(2)}, u32[]{:S(2)}) async-start(bf16[8,128,640]{2,1,0:T(8,128)(2,1)} %broadcast_in_dim.3), calls=%async_computation.2 | async-start | bytes 2621440 | tf_op jit(solution)/shard_map/all_to_all | solution.py:22
  80.7 12.4 %collective-permute-start.2 = (bf16[6,128,128]{2,1,0:T(8,128)(2,1)}, bf16[6,128,128]{2,1,0:T(8,128)(2,1)S(1)}, u32[]{:S(2)}, u32[]{:S(2)}) collective-permute-start(bf16[6,128,128]{2,1,0:T(8,128)(2,1)} %pack_queries.1.refs_0_), channel_id=1, source_target_pairs={{0,96},{32,0},{64,32},{96,64},{1,97},{33,1},{65,33},{97,65},{2,98}... | collective-permute-start | bytes 589832 | tf_op jit(solution)/shard_map/ppermute | solution.py:328
  85.3 11.0 %collective-permute-start.1 = (bf16[6,128,128]{2,1,0:T(8,128)(2,1)}, bf16[6,128,128]{2,1,0:T(8,128)(2,1)S(1)}, u32[]{:S(2)}, u32[]{:S(2)}) collective-permute-start(bf16[6,128,128]{2,1,0:T(8,128)(2,1)} %pack_queries.1.refs_0_), channel_id=1, source_target_pairs={{0,64},{32,96},{64,0},{96,32},{1,65},{33,97},{65,1},{97,33},{2,66}... | collective-permute-start | bytes 589832 | tf_op jit(solution)/shard_map/ppermute | solution.py:328
  88.0 10.3 %collective-permute-start = (bf16[6,128,128]{2,1,0:T(8,128)(2,1)}, bf16[6,128,128]{2,1,0:T(8,128)(2,1)S(1)}, u32[]{:S(2)}, u32[]{:S(2)}) collective-permute-start(bf16[6,128,128]{2,1,0:T(8,128)(2,1)} %pack_queries.1.refs_0_), channel_id=1, source_target_pairs={{0,32},{32,64},{64,96},{96,0},{1,33},{33,65},{65,97},{97,1},{2,34}... | collective-permute-start | bytes 589832 | tf_op jit(solution)/shard_map/ppermute | solution.py:328
  93.1 5.3 %copy-start.1 = (bf16[6,128,128]{2,1,0:T(8,128)(2,1)}, bf16[6,128,128]{2,1,0:T(8,128)(2,1)S(1)}, u32[]{:S(2)}) copy-start(bf16[6,128,128]{2,1,0:T(8,128)(2,1)S(1)} %collective-permute-done.2.refs_3_) | copy-start | bytes 589828
  96.3 2.0 %copy-start.2 = (bf16[6,128,128]{2,1,0:T(8,128)(2,1)}, bf16[6,128,128]{2,1,0:T(8,128)(2,1)S(1)}, u32[]{:S(2)}) copy-start(bf16[6,128,128]{2,1,0:T(8,128)(2,1)S(1)} %collective-permute-done.1.refs_2_) | copy-start | bytes 589828
  98.4 0.7 copy-start.3
  111.1 1.1 copy-start

commit v3 on v2

--- a/solution.py
+++ b/solution.py
@@ -14,6 +14,7 @@
 LANES = 128
 LOG2_E = 1.4426950408889634
 LOW = -1e30
+MIB = 1 << 20
 WHOLE = pl.BlockSpec(memory_space=pltpu.VMEM)
 SCALARS = pl.BlockSpec(memory_space=pltpu.SMEM)
 
@@ -47,6 +48,7 @@
         in_specs=[WHOLE],
         out_specs=WHOLE,
         cost_estimate=cost(0, 2 * slabs * tokens * LANES * 2),
+        compiler_params=pltpu.CompilerParams(vmem_limit_bytes=4 * MIB),
         name="pack_queries",
     )(query)
 
@@ -68,6 +70,7 @@
         in_specs=[WHOLE, WHOLE],
         out_specs=WHOLE,
         cost_estimate=cost(2 * tokens * depth * width, tokens * padded * 4),
+        compiler_params=pltpu.CompilerParams(vmem_limit_bytes=6 * MIB),
         name="project",
     )(section_in, w_down)
 
@@ -93,6 +96,7 @@
         in_specs=[WHOLE, WHOLE],
         out_specs=WHOLE,
         cost_estimate=cost(0, parts * rows * width * 8),
+        compiler_params=pltpu.CompilerParams(vmem_limit_bytes=4 * MIB),
         name="norm_rows",
     )(pieces, gain)
 
@@ -135,6 +139,7 @@
             2 * share * heads * tokens * LANES * latent,
             share * heads * tokens * (latent + LANES) * 4,
         ),
+        compiler_params=pltpu.CompilerParams(vmem_limit_bytes=6 * MIB),
         name="absorb",
     )(block_ids, place, *slabs, key_up)
 
@@ -266,6 +271,7 @@
         cost_estimate=cost(
             share * 6 * rows * n_keys * (width + latent), share * rows * width * 4
         ),
+        compiler_params=pltpu.CompilerParams(vmem_limit_bytes=24 * MIB),
         name="attend",
     )(block_ids, place, query_full, keys, value_up)
 
@@ -307,6 +313,7 @@
         in_specs=[SCALARS, SCALARS, WHOLE],
         out_specs=WHOLE,
         cost_estimate=cost(0, share * tokens * width * 2),
+        compiler_params=pltpu.CompilerParams(vmem_limit_bytes=6 * MIB),
         name="combine",
     )(block_ids, place, parts)
 

time: 142 us -> 136 us (0.958)
  Pallas kernels: 22.7 us -> 13.5 us
  local copies, waits for them, and re-layouts: 4.79 us -> 7.71 us
  waiting for transfers between devices: 16.3 us -> 19.1 us
    all_to_all x1, waiting for transfers between devices: 8.48 us -> 11.6 us  [exchange(): return lax.all_to_all(array, axes, 0, 0, tiled=True)]
    unnamed x12 -> x22, local copies, waits for them, and re-layouts: 3.62 us -> 6.53 us
    pallas_call x1, Pallas kernels: 3.63 us -> 1.24 us  [absorb(): pl.pallas_call(kernel, out_shape=jax.ShapeDtypeStruct((share, 2, heads *...]
    pallas_call x1, Pallas kernels: 2.13 us -> 0.27 us  [project(): pl.pallas_call(kernel, out_shape=jax.ShapeDtypeStruct((pieces, rows, padd...]
    pallas_call x1, Pallas kernels: 1.76 us -> 0.11 us  [norm_rows(): pl.pallas_call(kernel, out_shape=jax.ShapeDtypeStruct((copies, rows, late...]
    pallas_call x1, Pallas kernels: 2.08 us -> 0.46 us  [pack_queries(): pl.pallas_call(kernel, out_shape=jax.ShapeDtypeStruct((slabs, tokens, LAN...]
  transfers between devices with their start and end apart: 5 -> 5, of which waited for: 5 -> 5; matrix products, arithmetic and copies ran while one was open for 1% -> 0% of each run, Pallas kernels for 4% -> 1%
where the time goes in v3:
time: 136 us; the launch traced here: 135 us
  blocking collectives  75.7 us (56%)
  starting transfers between devices  19.1 us (14%)
  waiting for transfers between devices  19.1 us (14%)
  Pallas kernels  13.5 us (10%)
  local copies, waits for them, and re-layouts  7.71 us (6%)
    all_to_all x3, blocking collectives, exchange(): return lax.all_to_all(array, axes, 0, 0, tiled=True)  75.7 us
    all_to_all x1, waiting for transfers between devices, exchange(): return lax.all_to_all(array, axes, 0, 0, tiled=True)  11.6 us
    ppermute x3, starting transfers between devices, shards(): slabs.append(lax.ppermute(slabs[0], SHARE, pairs))  10.2 us
    pallas_call x1, Pallas kernels, attend(): pl.pallas_call(kernel, out_shape=jax.ShapeDtypeStruct((share, tokens, out...  9.52 us
    all_to_all x1, starting transfers between devices, exchange(): return lax.all_to_all(array, axes, 0, 0, tiled=True)  7.23 us
    unnamed x22, local copies, waits for them, and re-layouts  6.53 us
    ppermute x3, waiting for transfers between devices, shards(): slabs.append(lax.ppermute(slabs[0], SHARE, pairs))  6.52 us
  transfers between devices with their start and end apart: 5, of which 5 were waited for; matrix products, arithmetic and copies ran while one was open for 0% of the time, Pallas kernels for 1%

profile of v3, /device:TPU:64, one launch (start us, length us, event | category | flops | bytes accessed | tf_op | source)
XLA Modules:
  0.0 135.3 jit_solution(859956745667522072)
XLA Ops:
  0.0 1.0 copy.10
  1.0 1.7 %collective-permute-start.3 = (bf16[1,128,448]{2,1,0:T(8,128)(2,1)S(1)}, bf16[1,128,448]{2,1,0:T(8,128)(2,1)S(1)}, u32[]{:S(2)}, u32[]{:S(2)}) collective-permute-start(bf16[1,128,448]{2,1,0:T(8,128)(2,1)S(1)} %copy.10), channel_id=1, source_target_pairs={{0,16},{1,17},{2,18},{3,19},{4,20},{5,21},{6,22},{7,23},{8,24},{9,... | collective-permute-start | bytes 344072 | tf_op jit(solution)/shard_map/ppermute | solution.py:328
  2.8 1.0 collective-permute-done.3
  3.8 0.0 copy-start
  3.8 1.1 copy-done
  4.8 0.3 project.1
  5.1 38.8 %all_to_all.20.pieces_ref = f32[16,8,640]{2,1,0:T(8,128)S(1)} all-to-all(f32[16,8,640]{2,1,0:T(8,128)S(1)} %project.1), channel_id=1, replica_groups=mesh['y'=8,'x'=4,'pp'=2,'tp'=16] {'tp'}, dimensions={0} | all-to-all | bytes 655360 | tf_op jit(solution)/shard_map/all_to_all | solution.py:23
  43.9 0.0 copy-done.6
  43.9 0.1 norm_rows.1
  44.0 21.8 %all_to_all.21 = bf16[16,8,640]{2,1,0:T(8,128)(2,1)S(1)} all-to-all(bf16[16,8,640]{2,1,0:T(8,128)(2,1)S(1)} %norm_rows.1), channel_id=1, replica_groups=mesh['y'=8,'x'=4,'pp'=2,'tp'=16] {'tp'}, dimensions={0} | all-to-all | bytes 327680 | tf_op jit(solution)/shard_map/all_to_all | solution.py:23
  65.7 1.2 broadcast_in_dim.3
  66.9 7.2 %all-to-all-start.2 = ((bf16[8,128,640]{2,1,0:T(8,128)(2,1)}), bf16[8,128,640]{2,1,0:T(8,128)(2,1)}, u32[]{:S(2)}, u32[]{:S(2)}) async-start(bf16[8,128,640]{2,1,0:T(8,128)(2,1)} %broadcast_in_dim.3), calls=%async_computation.2 | async-start | bytes 2621440 | tf_op jit(solution)/shard_map/all_to_all | solution.py:23
  74.1 0.0 copy-done.9
  74.1 0.2 copy.8
  74.3 0.5 pack_queries.1.refs_0_
  74.8 4.7 %collective-permute-start.2 = (bf16[6,128,128]{2,1,0:T(8,128)(2,1)S(1)}, bf16[6,128,128]{2,1,0:T(8,128)(2,1)S(1)}, u32[]{:S(2)}, u32[]{:S(2)}) collective-permute-start(bf16[6,128,128]{2,1,0:T(8,128)(2,1)S(1)} %pack_queries.1.refs_0_), channel_id=1, source_target_pairs={{0,96},{32,0},{64,32},{96,64},{1,97},{33,1},{65,33},{97,65},{2,98}... | collective-permute-start | bytes 589832 | tf_op jit(solution)/shard_map/ppermute | solution.py:335
  79.5 2.7 %collective-permute-start.1 = (bf16[6,128,128]{2,1,0:T(8,128)(2,1)S(1)}, bf16[6,128,128]{2,1,0:T(8,128)(2,1)S(1)}, u32[]{:S(2)}, u32[]{:S(2)}) collective-permute-start(bf16[6,128,128]{2,1,0:T(8,128)(2,1)S(1)} %pack_queries.1.refs_0_), channel_id=1, source_target_pairs={{0,64},{32,96},{64,0},{96,32},{1,65},{33,97},{65,1},{97,33},{2,66}... | collective-permute-start | bytes 589832 | tf_op jit(solution)/shard_map/ppermute | solution.py:335
  82.2 2.8 %collective-permute-start = (bf16[6,128,128]{2,1,0:T(8,128)(2,1)S(1)}, bf16[6,128,128]{2,1,0:T(8,128)(2,1)S(1)}, u32[]{:S(2)}, u32[]{:S(2)}) collective-permute-start(bf16[6,128,128]{2,1,0:T(8,128)(2,1)S(1)} %pack_queries.1.refs_0_), channel_id=1, source_target_pairs={{0,32},{32,64},{64,96},{96,0},{1,33},{33,65},{65,97},{97,1},{2,34}... | collective-permute-start | bytes 589832 | tf_op jit(solution)/shard_map/ppermute | solution.py:335
  85.0 0.1 pad_add_fusion.place_ref
  85.1 1.8 %collective-permute-done.2.refs_3_ = bf16[6,128,128]{2,1,0:T(8,128)(2,1)S(1)} collective-permute-done((bf16[6,128,128]{2,1,0:T(8,128)(2,1)S(1)}, bf16[6,128,128]{2,1,0:T(8,128)(2,1)S(1)}, u32[]{:S(2)}, u32[]{:S(2)}) %collective-permute-start.2) | collective-permute-done | bytes 196640 | tf_op jit(solution)/shard_map/ppermute | solution.py:335
  86.9 3.3 %collective-permute-done.1.refs_2_ = bf16[6,128,128]{2,1,0:T(8,128)(2,1)S(1)} collective-permute-done((bf16[6,128,128]{2,1,0:T(8,128)(2,1)S(1)}, bf16[6,128,128]{2,1,0:T(8,128)(2,1)S(1)}, u32[]{:S(2)}, u32[]{:S(2)}) %collective-permute-start.1) | collective-permute-done | bytes 196640 | tf_op jit(solution)/shard_map/ppermute | solution.py:335
  90.2 0.7 copy-done.2
  90.9 1.4 %collective-permute-done.refs_1_ = bf16[6,128,128]{2,1,0:T(8,128)(2,1)S(1)} collective-permute-done((bf16[6,128,128]{2,1,0:T(8,128)(2,1)S(1)}, bf16[6,128,128]{2,1,0:T(8,128)(2,1)S(1)}, u32[]{:S(2)}, u32[]{:S(2)}) %collective-permute-start) | collective-permute-done | bytes 196640 | tf_op jit(solution)/shard_map/ppermute | solution.py:335
  92.3 0.7 copy-done.4
  93.0 0.9 copy-done.3
  93.9 0.9 copy-done.5
  94.8 1.2 absorb.1.query_ref
  96.1 11.6 %all-to-all-done.2.keys_ref = bf16[8,128,640]{2,1,0:T(8,128)(2,1)} async-done(((bf16[8,128,640]{2,1,0:T(8,128)(2,1)}), bf16[8,128,640]{2,1,0:T(8,128)(2,1)}, u32[]{:S(2)}, u32[]{:S(2)}) %all-to-all-start.2) | async-done | bytes 1310752 | tf_op jit(solution)/shard_map/all_to_all | solution.py:23
  107.7 1.0 copy-done.8
  108.7 9.5 %attend.1 = bf16[4,128,640]{2,1,0:T(8,128)(2,1)S(1)} custom-call(s32[64]{0:T(128)S(1)} %copy-done.7, s32[3]{0:T(128)S(1)} %pad_add_fusion.place_ref, bf16[4,2,256,640]{3,2,1,0:T(8,128)(2,1)S(1)} %absorb.1.query_ref, bf16[8,128,640]{2,1,0:T(8,128)(2,1)} %all-to-all-done.2.keys_ref, bf16[4,512,128]{2,1,0:T(8,128)(2,1)S(1)} %bitcast.12), custom_call_target="tpu_custom_call" | custom-call | flops 3623878656 | bytes 2621440 | tf_op jit(solution)/shard_map/attend/pallas_call | solution.py:253
  118.2 15.2 %all_to_all.22.parts_ref = bf16[4,128,640]{2,1,0:T(8,128)(2,1)S(1)} all-to-all(bf16[4,128,640]{2,1,0:T(8,128)(2,1)S(1)} %attend.1), channel_id=1, replica_groups=mesh['y'=8,'x'=4,'pp'=2,'tp'=16] {'x'}, dimensions={0} | all-to-all | bytes 1310720 | tf_op jit(solution)/shard_map/all_to_all | solution.py:23
  133.4 1.9 %combine.1 = bf16[1,128,512]{2,1,0:T(8,128)(2,1)} custom-call(s32[64]{0:T(128)S(1)} %copy-done.7, s32[3]{0:T(128)S(1)} %pad_add_fusion.place_ref, bf16[4,128,640]{2,1,0:T(8,128)(2,1)S(1)} %all_to_all.22.parts_ref), custom_call_target="tpu_custom_call" | custom-call | bytes 655360 | tf_op jit(solution)/shard_map/combine/pallas_call | solution.py:310
  (12 shorter events, 0.0 us)
Async XLA Ops:
  0.0 43.9 %copy-start.6 = (f32[1,512]{1,0:T(1,128)S(1)}, f32[1,512]{1,0:T(1,128)}, u32[]{:S(2)}) copy-start(f32[1,512]{1,0:T(1,128)} %gain_ref.1) | copy-start | bytes 6148
  1.0 2.7 %collective-permute-start.3 = (bf16[1,128,448]{2,1,0:T(8,128)(2,1)S(1)}, bf16[1,128,448]{2,1,0:T(8,128)(2,1)S(1)}, u32[]{:S(2)}, u32[]{:S(2)}) collective-permute-start(bf16[1,128,448]{2,1,0:T(8,128)(2,1)S(1)} %copy.10), channel_id=1, source_target_pairs={{0,16},{1,17},{2,18},{3,19},{4,20},{5,21},{6,22},{7,23},{8,24},{9,... | collective-permute-start | bytes 344072 | tf_op jit(solution)/shard_map/ppermute | solution.py:328
  3.8 1.1 copy-start
  66.9 7.2 %copy-start.9 = (bf16[1,128,4,192]{1,3,2,0:T(8,128)(2,1)S(1)}, bf16[1,128,4,192]{1,3,2,0:T(8,128)(2,1)}, u32[]{:S(2)}) copy-start(bf16[1,128,4,192]{1,3,2,0:T(8,128)(2,1)} %param.10) | copy-start | bytes 589828
  66.9 26.1 %copy-start.1 = (bf16[1,4,128,512]{3,2,1,0:T(8,128)(2,1)S(1)}, bf16[1,4,128,512]{3,2,1,0:T(8,128)(2,1)}, u32[]{:S(2)}) copy-start(bf16[1,4,128,512]{3,2,1,0:T(8,128)(2,1)} %param.11) | copy-start | bytes 1572868
  66.9 26.1 %copy-start.7 = (s32[64]{0:T(128)S(1)}, s32[64]{0:T(128)}, u32[]{:S(2)}) copy-start(s32[64]{0:T(128)} %ids_ref.5) | copy-start | bytes 772
  66.9 40.8 %all-to-all-start.2 = ((bf16[8,128,640]{2,1,0:T(8,128)(2,1)}), bf16[8,128,640]{2,1,0:T(8,128)(2,1)}, u32[]{:S(2)}, u32[]{:S(2)}) async-start(bf16[8,128,640]{2,1,0:T(8,128)(2,1)} %broadcast_in_dim.3), calls=%async_computation.2 | async-start | bytes 2621440 | tf_op jit(solution)/shard_map/all_to_all | solution.py:23
  74.8 12.1 %collective-permute-start.2 = (bf16[6,128,128]{2,1,0:T(8,128)(2,1)S(1)}, bf16[6,128,128]{2,1,0:T(8,128)(2,1)S(1)}, u32[]{:S(2)}, u32[]{:S(2)}) collective-permute-start(bf16[6,128,128]{2,1,0:T(8,128)(2,1)S(1)} %pack_queries.1.refs_0_), channel_id=1, source_target_pairs={{0,96},{32,0},{64,32},{96,64},{1,97},{33,1},{65,33},{97,65},{2,98}... | collective-permute-start | bytes 589832 | tf_op jit(solution)/shard_map/ppermute | solution.py:335
  79.5 10.8 %collective-permute-start.1 = (bf16[6,128,128]{2,1,0:T(8,128)(2,1)S(1)}, bf16[6,128,128]{2,1,0:T(8,128)(2,1)S(1)}, u32[]{:S(2)}, u32[]{:S(2)}) collective-permute-start(bf16[6,128,128]{2,1,0:T(8,128)(2,1)S(1)} %pack_queries.1.refs_0_), channel_id=1, source_target_pairs={{0,64},{32,96},{64,0},{96,32},{1,65},{33,97},{65,1},{97,33},{2,66}... | collective-permute-start | bytes 589832 | tf_op jit(solution)/shard_map/ppermute | solution.py:335
  82.2 10.1 %collective-permute-start = (bf16[6,128,128]{2,1,0:T(8,128)(2,1)S(1)}, bf16[6,128,128]{2,1,0:T(8,128)(2,1)S(1)}, u32[]{:S(2)}, u32[]{:S(2)}) collective-permute-start(bf16[6,128,128]{2,1,0:T(8,128)(2,1)S(1)} %pack_queries.1.refs_0_), channel_id=1, source_target_pairs={{0,32},{32,64},{64,96},{96,0},{1,33},{33,65},{65,97},{97,1},{2,34}... | collective-permute-start | bytes 589832 | tf_op jit(solution)/shard_map/ppermute | solution.py:335
  90.2 0.7 copy-start.2
  92.3 0.7 copy-start.4
  93.0 0.9 copy-start.3
  93.9 0.9 copy-start.5
  107.7 1.0 copy-start.8

commit v4 on v3

--- a/solution.py
+++ b/solution.py
@@ -8,9 +8,9 @@
 from jax.sharding import Mesh
 from jax.sharding import PartitionSpec as P
 
-CTX = ("y", "x")
-SHARE = "x"
-KEYS = "y"
+CTX = ("y1", "y0", "x")
+SHARE = "y1"
+KEYS = ("y0", "x")
 LANES = 128
 LOG2_E = 1.4426950408889634
 LOW = -1e30
@@ -111,7 +111,7 @@
     def kernel(ids_ref, place_ref, *refs):
         slab_refs, up_ref, out_ref = refs[:share], refs[share], refs[share + 1]
         for back, slab_ref in enumerate(slab_refs):
-            owner = place_ref[0] + lax.rem(place_ref[1] + share - back, share)
+            owner = place_ref[0] + lax.rem(place_ref[1] + share - back, share) * place_ref[2]
             first = (ids_ref[2 * owner] >= n_blocks // 2).astype(jnp.int32)
             for head in range(heads):
                 value = jnp.dot(
@@ -161,7 +161,7 @@
             spot = lax.broadcasted_iota(jnp.int32, (8, n_keys), 1)
             low_pos = spot
             for source in range(sources):
-                owner = place_ref[1] + source * place_ref[2]
+                owner = place_ref[1] * sources + source
                 id_first = ids_ref[2 * owner]
                 first = (id_first >= n_blocks // 2).astype(jnp.int32)
                 low_id = jnp.minimum(id_first, n_blocks - 1 - id_first)
@@ -181,7 +181,7 @@
                 turned[side] = plain[side].T
 
         receiver = lax.rem(place_ref[1] + share - step, share)
-        id_first = ids_ref[2 * (place_ref[0] + receiver)]
+        id_first = ids_ref[2 * (place_ref[0] + receiver * sources)]
         low_id = jnp.minimum(id_first, n_blocks - 1 - id_first)
         within = lax.broadcasted_iota(jnp.int32, (rows, 1), 0) % half
 
@@ -193,15 +193,20 @@
 
         def masked(side, block):
             seen = key_pos[side, 0:1, :] <= block * half + within
-            return seen, jnp.where(seen, score(side, side), LOW)
+            return jnp.where(seen, score(side, side), LOW)
+
+        def weigh(expo, key_side):
+            return jnp.dot(
+                expo.astype(jnp.bfloat16),
+                plain[key_side, :, :latent],
+                preferred_element_type=jnp.float32,
+            )
 
         lane = lax.broadcasted_iota(jnp.int32, (half, LANES), 1)
 
         def finish(side, top, total, weighted):
-            some = total > 0.0
-            safe = jnp.where(some, total, 1.0)
-            value = (weighted * (1.0 / safe)).astype(jnp.bfloat16)
-            level = jnp.where(some, top + jnp.log2(safe), LOW)
+            value = (weighted * (1.0 / total)).astype(jnp.bfloat16)
+            level = jnp.where(top > 0.5 * LOW, top + jnp.log2(total), LOW)
             high = level.astype(jnp.bfloat16).astype(jnp.float32)
             rest = level - high
             middle = rest.astype(jnp.bfloat16).astype(jnp.float32)
@@ -215,31 +220,22 @@
                     tile = jnp.where(lane == 3 * head + at, part[span], tile)
             out_ref[receiver, pl.ds(side * half, half), heads * value_dim :] = tile.astype(jnp.bfloat16)
 
-        seen, low_low = masked(0, low_id)
-        top = jnp.max(low_low, axis=1, keepdims=True)
-        expo = jnp.where(seen, jnp.exp2(low_low - top), 0.0)
-        total = jnp.sum(expo, axis=1, keepdims=True)
-        weighted = jnp.dot(
-            expo.astype(jnp.bfloat16), plain[0, :, :latent], preferred_element_type=jnp.float32
-        )
-        finish(0, top, total, weighted)
-
+        low_low = masked(0, low_id)
         high_low = score(1, 0)
-        seen, high_high = masked(1, n_blocks - 1 - low_id)
-        top = jnp.maximum(
+        high_high = masked(1, n_blocks - 1 - low_id)
+        top_low = jnp.max(low_low, axis=1, keepdims=True)
+        top_high = jnp.maximum(
             jnp.max(high_low, axis=1, keepdims=True), jnp.max(high_high, axis=1, keepdims=True)
         )
-        expo_low = jnp.exp2(high_low - top)
-        expo_high = jnp.where(seen, jnp.exp2(high_high - top), 0.0)
-        total = jnp.sum(expo_low, axis=1, keepdims=True) + jnp.sum(
-            expo_high, axis=1, keepdims=True
+        low_low = jnp.exp2(low_low - top_low)
+        high_low = jnp.exp2(high_low - top_high)
+        high_high = jnp.exp2(high_high - top_high)
+        total_low = jnp.sum(low_low, axis=1, keepdims=True)
+        total_high = jnp.sum(high_low, axis=1, keepdims=True) + jnp.sum(
+            high_high, axis=1, keepdims=True
         )
-        weighted = jnp.dot(
-            expo_low.astype(jnp.bfloat16), plain[0, :, :latent], preferred_element_type=jnp.float32
-        ) + jnp.dot(
-            expo_high.astype(jnp.bfloat16), plain[1, :, :latent], preferred_element_type=jnp.float32
-        )
-        finish(1, top, total, weighted)
+        finish(0, top_low, total_low, weigh(low_low, 0))
+        finish(1, top_high, total_high, weigh(high_low, 0) + weigh(high_high, 1))
 
         @pl.when(step == share - 1)
         def _():
@@ -284,7 +280,7 @@
     n_blocks = block_ids.shape[0]
 
     def kernel(ids_ref, place_ref, parts_ref, out_ref):
-        first = (ids_ref[2 * (place_ref[0] + place_ref[1])] >= n_blocks // 2).astype(jnp.int32)
+        first = (ids_ref[2 * (place_ref[0] + place_ref[1] * place_ref[2])] >= n_blocks // 2).astype(jnp.int32)
         for side in range(2):
             begin = pl.multiple_of(jnp.where(first == side, 0, half), half)
             span = slice(side * half, (side + 1) * half)
@@ -320,10 +316,11 @@
 
 def shards(outgoing, w_down, kv_gain, queries, w_key_up, w_value_up, block_ids):
     section_idx = lax.axis_index("pp")
-    n_share, n_keys, tp_size = (lax.axis_size(a) for a in (SHARE, KEYS, "tp"))
+    n_share, n_y0, n_x, tp_size = (lax.axis_size(a) for a in (SHARE, *KEYS, "tp"))
+    n_keys = n_y0 * n_x
     tokens, heads, query_dim = queries.shape[1:]
-    y, x = (lax.axis_index(a).astype(jnp.int32) for a in CTX)
-    place = jnp.stack([y * n_share, x, jnp.int32(n_share)])
+    y1, y0, x = (lax.axis_index(a).astype(jnp.int32) for a in CTX)
+    place = jnp.stack([y0 * n_x + x, y1, jnp.int32(n_keys)])
 
     moved = lax.ppermute(outgoing, "pp", [(0, 1)])
     section_in = jnp.where(section_idx == 0, outgoing, moved)[0]
@@ -336,7 +333,7 @@
     local = norm_rows(pieces, kv_gain, tp_size)
     key_rows = exchange(local, ("tp",)).reshape(tokens, -1)
     query_full = absorb(block_ids, place, slabs, w_key_up[0])
-    keys = exchange(jnp.broadcast_to(key_rows, (n_keys, *key_rows.shape)), (KEYS,))
+    keys = exchange(jnp.broadcast_to(key_rows, (n_keys, *key_rows.shape)), KEYS)
     part_out = attend(block_ids, place, query_full, keys, w_value_up[0], query_dim**-0.5)
     got = exchange(part_out, (SHARE,))
     return combine(block_ids, place, got, heads)
@@ -359,7 +356,7 @@
 
 def solution(mesh):
     torus = Mesh(
-        mesh.devices.reshape(8, 4, mesh.shape["pp"], mesh.shape["tp"]),
-        ("y", "x", "pp", "tp"),
+        mesh.devices.reshape(4, 2, 4, mesh.shape["pp"], mesh.shape["tp"]),
+        ("y1", "y0", "x", "pp", "tp"),
     )
     return build(torus)

time: 136 us -> 142 us (1.044)
  the two profiles are of different devices: /device:TPU:64 before, /device:TPU:72 now
where the time goes in v4:
time: 142 us
  blocking collectives  78.7 us (55%)
  waiting for transfers between devices  21.8 us (15%)
  starting transfers between devices  21.2 us (15%)
  Pallas kernels  12.2 us (9%)
  local copies, waits for them, and re-layouts  7.7 us (5%)
    all_to_all x3, blocking collectives, exchange(): return lax.all_to_all(array, axes, 0, 0, tiled=True)  78.7 us
    ppermute x3, waiting for transfers between devices, shards(): slabs.append(lax.ppermute(slabs[0], SHARE, pairs))  20.9 us
    ppermute x3, starting transfers between devices, shards(): slabs.append(lax.ppermute(slabs[0], SHARE, pairs))  13.6 us
    pallas_call x1, Pallas kernels, attend(): pl.pallas_call(kernel, out_shape=jax.ShapeDtypeStruct((share, tokens, out...  8.27 us
    unnamed x22, local copies, waits for them, and re-layouts  6.53 us
    all_to_all x1, starting transfers between devices, exchange(): return lax.all_to_all(array, axes, 0, 0, tiled=True)  5.89 us
  transfers between devices with their start and end apart: 5, of which 3 were waited for; matrix products, arithmetic and copies ran while one was open for 0% of the time, Pallas kernels for 1%

profile of v4, /device:TPU:72, one launch (start us, length us, event | category | flops | bytes accessed | tf_op | source)
XLA Modules:
  0.0 141.9 jit_solution(7366360662011609869)
XLA Ops:
  0.0 1.0 copy.10
  1.0 1.7 %collective-permute-start.3 = (bf16[1,128,448]{2,1,0:T(8,128)(2,1)S(1)}, bf16[1,128,448]{2,1,0:T(8,128)(2,1)S(1)}, u32[]{:S(2)}, u32[]{:S(2)}) collective-permute-start(bf16[1,128,448]{2,1,0:T(8,128)(2,1)S(1)} %copy.10), channel_id=1, source_target_pairs={{0,16},{1,17},{2,18},{3,19},{4,20},{5,21},{6,22},{7,23},{8,24},{9,... | collective-permute-start | bytes 344072 | tf_op jit(solution)/shard_map/ppermute | solution.py:325
  2.8 1.0 collective-permute-done.3
  3.8 0.0 copy-start
  3.8 1.1 copy-done
  4.8 0.3 project.1
  5.1 38.8 %all_to_all.20.pieces_ref = f32[16,8,640]{2,1,0:T(8,128)S(1)} all-to-all(f32[16,8,640]{2,1,0:T(8,128)S(1)} %project.1), channel_id=1, replica_groups=mesh['y1'=4,'y0'=2,'x'=4,'pp'=2,'tp'=16] {'tp'}, dimensions={0} | all-to-all | bytes 655360 | tf_op jit(solution)/shard_map/all_to_all | solution.py:23
  43.8 0.0 copy-done.6
  43.8 0.1 norm_rows.1
  44.0 21.8 %all_to_all.21 = bf16[16,8,640]{2,1,0:T(8,128)(2,1)S(1)} all-to-all(bf16[16,8,640]{2,1,0:T(8,128)(2,1)S(1)} %norm_rows.1), channel_id=1, replica_groups=mesh['y1'=4,'y0'=2,'x'=4,'pp'=2,'tp'=16] {'tp'}, dimensions={0} | all-to-all | bytes 327680 | tf_op jit(solution)/shard_map/all_to_all | solution.py:23
  65.7 1.2 broadcast_in_dim.3
  66.9 5.9 %all-to-all-start.2 = ((bf16[8,128,640]{2,1,0:T(8,128)(2,1)}), bf16[8,128,640]{2,1,0:T(8,128)(2,1)}, u32[]{:S(2)}, u32[]{:S(2)}) async-start(bf16[8,128,640]{2,1,0:T(8,128)(2,1)} %broadcast_in_dim.3), calls=%async_computation.2 | async-start | bytes 2621440 | tf_op jit(solution)/shard_map/all_to_all | solution.py:23
  72.8 0.2 copy.8
  73.0 0.5 pack_queries.1.refs_0_
  73.5 5.3 %collective-permute-start.2 = (bf16[6,128,128]{2,1,0:T(8,128)(2,1)S(1)}, bf16[6,128,128]{2,1,0:T(8,128)(2,1)S(1)}, u32[]{:S(2)}, u32[]{:S(2)}) collective-permute-start(bf16[6,128,128]{2,1,0:T(8,128)(2,1)S(1)} %pack_queries.1.refs_0_), channel_id=1, source_target_pairs={{0,768},{256,0},{512,256},{768,512},{1,769},{257,1},{513,257},{769... | collective-permute-start | bytes 589832 | tf_op jit(solution)/shard_map/ppermute | solution.py:332
  78.7 4.7 %collective-permute-start.1 = (bf16[6,128,128]{2,1,0:T(8,128)(2,1)S(1)}, bf16[6,128,128]{2,1,0:T(8,128)(2,1)S(1)}, u32[]{:S(2)}, u32[]{:S(2)}) collective-permute-start(bf16[6,128,128]{2,1,0:T(8,128)(2,1)S(1)} %pack_queries.1.refs_0_), channel_id=1, source_target_pairs={{0,512},{256,768},{512,0},{768,256},{1,513},{257,769},{513,1},{769... | collective-permute-start | bytes 589832 | tf_op jit(solution)/shard_map/ppermute | solution.py:332
  83.5 3.6 %collective-permute-start = (bf16[6,128,128]{2,1,0:T(8,128)(2,1)S(1)}, bf16[6,128,128]{2,1,0:T(8,128)(2,1)S(1)}, u32[]{:S(2)}, u32[]{:S(2)}) collective-permute-start(bf16[6,128,128]{2,1,0:T(8,128)(2,1)S(1)} %pack_queries.1.refs_0_), channel_id=1, source_target_pairs={{0,256},{256,512},{512,768},{768,0},{1,257},{257,513},{513,769},{7... | collective-permute-start | bytes 589832 | tf_op jit(solution)/shard_map/ppermute | solution.py:332
  87.1 0.1 pad_add_fusion.place_ref
  87.1 13.4 %collective-permute-done.2.refs_3_ = bf16[6,128,128]{2,1,0:T(8,128)(2,1)S(1)} collective-permute-done((bf16[6,128,128]{2,1,0:T(8,128)(2,1)S(1)}, bf16[6,128,128]{2,1,0:T(8,128)(2,1)S(1)}, u32[]{:S(2)}, u32[]{:S(2)}) %collective-permute-start.2) | collective-permute-done | bytes 196640 | tf_op jit(solution)/shard_map/ppermute | solution.py:332
  100.5 7.5 %collective-permute-done.1.refs_2_ = bf16[6,128,128]{2,1,0:T(8,128)(2,1)S(1)} collective-permute-done((bf16[6,128,128]{2,1,0:T(8,128)(2,1)S(1)}, bf16[6,128,128]{2,1,0:T(8,128)(2,1)S(1)}, u32[]{:S(2)}, u32[]{:S(2)}) %collective-permute-start.1) | collective-permute-done | bytes 196640 | tf_op jit(solution)/shard_map/ppermute | solution.py:332
  108.0 0.7 copy-done.2
  108.7 0.0 collective-permute-done.refs_1_
  108.7 0.7 copy-done.4
  109.4 0.9 copy-done.3
  110.3 0.9 copy-done.5
  111.2 1.2 absorb.1.query_ref
  112.5 0.0 all-to-all-done.2.keys_ref
  112.5 0.0 copy-start.8
  112.5 1.0 copy-done.8
  113.5 8.3 %attend.1 = bf16[4,128,640]{2,1,0:T(8,128)(2,1)S(1)} custom-call(s32[64]{0:T(128)S(1)} %copy-done.7, s32[3]{0:T(128)S(1)} %pad_add_fusion.place_ref, bf16[4,2,256,640]{3,2,1,0:T(8,128)(2,1)S(1)} %absorb.1.query_ref, bf16[8,128,640]{2,1,0:T(8,128)(2,1)} %all-to-all-done.2.keys_ref, bf16[4,512,128]{2,1,0:T(8,128)(2,1)S(1)} %bitcast.12), custom_call_target="tpu_custom_call" | custom-call | flops 3623878656 | bytes 2621440 | tf_op jit(solution)/shard_map/attend/pallas_call | solution.py:249
  121.8 18.2 %all_to_all.22.parts_ref = bf16[4,128,640]{2,1,0:T(8,128)(2,1)S(1)} all-to-all(bf16[4,128,640]{2,1,0:T(8,128)(2,1)S(1)} %attend.1), channel_id=1, replica_groups=mesh['y1'=4,'y0'=2,'x'=4,'pp'=2,'tp'=16] {'y1'}, dimensions={0} | all-to-all | bytes 1310720 | tf_op jit(solution)/shard_map/all_to_all | solution.py:23
  140.0 1.9 %combine.1 = bf16[1,128,512]{2,1,0:T(8,128)(2,1)} custom-call(s32[64]{0:T(128)S(1)} %copy-done.7, s32[3]{0:T(128)S(1)} %pad_add_fusion.place_ref, bf16[4,128,640]{2,1,0:T(8,128)(2,1)S(1)} %all_to_all.22.parts_ref), custom_call_target="tpu_custom_call" | custom-call | bytes 655360 | tf_op jit(solution)/shard_map/combine/pallas_call | solution.py:306
  (12 shorter events, 0.0 us)
Async XLA Ops:
  0.0 43.8 %copy-start.6 = (f32[1,512]{1,0:T(1,128)S(1)}, f32[1,512]{1,0:T(1,128)}, u32[]{:S(2)}) copy-start(f32[1,512]{1,0:T(1,128)} %gain_ref.1) | copy-start | bytes 6148
  1.0 2.7 %collective-permute-start.3 = (bf16[1,128,448]{2,1,0:T(8,128)(2,1)S(1)}, bf16[1,128,448]{2,1,0:T(8,128)(2,1)S(1)}, u32[]{:S(2)}, u32[]{:S(2)}) collective-permute-start(bf16[1,128,448]{2,1,0:T(8,128)(2,1)S(1)} %copy.10), channel_id=1, source_target_pairs={{0,16},{1,17},{2,18},{3,19},{4,20},{5,21},{6,22},{7,23},{8,24},{9,... | collective-permute-start | bytes 344072 | tf_op jit(solution)/shard_map/ppermute | solution.py:325
  3.8 1.1 copy-start
  66.9 5.9 %copy-start.9 = (bf16[1,128,4,192]{1,3,2,0:T(8,128)(2,1)S(1)}, bf16[1,128,4,192]{1,3,2,0:T(8,128)(2,1)}, u32[]{:S(2)}) copy-start(bf16[1,128,4,192]{1,3,2,0:T(8,128)(2,1)} %param.10) | copy-start | bytes 589828
  66.9 42.5 %copy-start.1 = (bf16[1,4,128,512]{3,2,1,0:T(8,128)(2,1)S(1)}, bf16[1,4,128,512]{3,2,1,0:T(8,128)(2,1)}, u32[]{:S(2)}) copy-start(bf16[1,4,128,512]{3,2,1,0:T(8,128)(2,1)} %param.11) | copy-start | bytes 1572868
  66.9 42.5 %copy-start.7 = (s32[64]{0:T(128)S(1)}, s32[64]{0:T(128)}, u32[]{:S(2)}) copy-start(s32[64]{0:T(128)} %ids_ref.5) | copy-start | bytes 772
  66.9 45.6 %all-to-all-start.2 = ((bf16[8,128,640]{2,1,0:T(8,128)(2,1)}), bf16[8,128,640]{2,1,0:T(8,128)(2,1)}, u32[]{:S(2)}, u32[]{:S(2)}) async-start(bf16[8,128,640]{2,1,0:T(8,128)(2,1)} %broadcast_in_dim.3), calls=%async_computation.2 | async-start | bytes 2621440 | tf_op jit(solution)/shard_map/all_to_all | solution.py:23
  73.5 27.1 %collective-permute-start.2 = (bf16[6,128,128]{2,1,0:T(8,128)(2,1)S(1)}, bf16[6,128,128]{2,1,0:T(8,128)(2,1)S(1)}, u32[]{:S(2)}, u32[]{:S(2)}) collective-permute-start(bf16[6,128,128]{2,1,0:T(8,128)(2,1)S(1)} %pack_queries.1.refs_0_), channel_id=1, source_target_pairs={{0,768},{256,0},{512,256},{768,512},{1,769},{257,1},{513,257},{769... | collective-permute-start | bytes 589832 | tf_op jit(solution)/shard_map/ppermute | solution.py:332
  78.7 29.3 %collective-permute-start.1 = (bf16[6,128,128]{2,1,0:T(8,128)(2,1)S(1)}, bf16[6,128,128]{2,1,0:T(8,128)(2,1)S(1)}, u32[]{:S(2)}, u32[]{:S(2)}) collective-permute-start(bf16[6,128,128]{2,1,0:T(8,128)(2,1)S(1)} %pack_queries.1.refs_0_), channel_id=1, source_target_pairs={{0,512},{256,768},{512,0},{768,256},{1,513},{257,769},{513,1},{769... | collective-permute-start | bytes 589832 | tf_op jit(solution)/shard_map/ppermute | solution.py:332
  83.5 25.2 %collective-permute-start = (bf16[6,128,128]{2,1,0:T(8,128)(2,1)S(1)}, bf16[6,128,128]{2,1,0:T(8,128)(2,1)S(1)}, u32[]{:S(2)}, u32[]{:S(2)}) collective-permute-start(bf16[6,128,128]{2,1,0:T(8,128)(2,1)S(1)} %pack_queries.1.refs_0_), channel_id=1, source_target_pairs={{0,256},{256,512},{512,768},{768,0},{1,257},{257,513},{513,769},{7... | collective-permute-start | bytes 589832 | tf_op jit(solution)/shard_map/ppermute | solution.py:332
  108.0 0.7 copy-start.2
  108.7 0.7 copy-start.4
  109.4 0.9 copy-start.3
  110.3 0.9 copy-start.5
  112.5 1.0 copy-start.8

commit v5 on v4

--- a/solution.py
+++ b/solution.py
@@ -4,6 +4,7 @@
 import jax.numpy as jnp
 from jax import lax
 from jax.experimental import pallas as pl
+from jax.experimental.layout import Layout, with_layout_constraint
 from jax.experimental.pallas import tpu as pltpu
 from jax.sharding import Mesh
 from jax.sharding import PartitionSpec as P
@@ -12,6 +13,7 @@
 SHARE = "y1"
 KEYS = ("y0", "x")
 LANES = 128
+SUBLANES = 8
 LOG2_E = 1.4426950408889634
 LOW = -1e30
 MIB = 1 << 20
@@ -25,54 +27,6 @@
 
 def cost(flops, bytes_accessed):
     return pl.CostEstimate(flops=flops, bytes_accessed=bytes_accessed, transcendentals=0)
-
-
-def pack_queries(query):
-    tokens, heads, width = query.shape
-    nope = LANES
-    rope = width - nope
-    slabs = heads + heads * rope // LANES
-
-    def kernel(query_ref, out_ref):
-        rows = query_ref[...]
-        for head in range(heads):
-            out_ref[head] = rows[:, head, :nope]
-        for pair in range(heads // 2):
-            out_ref[heads + pair] = jnp.concatenate(
-                [rows[:, 2 * pair, nope:], rows[:, 2 * pair + 1, nope:]], axis=-1
-            )
-
-    return pl.pallas_call(
-        kernel,
-        out_shape=jax.ShapeDtypeStruct((slabs, tokens, LANES), query.dtype),
-        in_specs=[WHOLE],
-        out_specs=WHOLE,
-        cost_estimate=cost(0, 2 * slabs * tokens * LANES * 2),
-        compiler_params=pltpu.CompilerParams(vmem_limit_bytes=4 * MIB),
-        name="pack_queries",
-    )(query)
-
-
-def project(section_in, w_down, pieces):
-    tokens, depth = section_in.shape
-    width = w_down.shape[-1]
-    padded = -(-width // LANES) * LANES
-    rows = tokens // pieces
-
-    def kernel(in_ref, down_ref, out_ref):
-        value = jnp.dot(in_ref[...], down_ref[...], preferred_element_type=jnp.float32)
-        out_ref[:, :, :width] = value.reshape(pieces, rows, width)
-        out_ref[:, :, width:] = jnp.zeros((pieces, rows, padded - width), jnp.float32)
-
-    return pl.pallas_call(
-        kernel,
-        out_shape=jax.ShapeDtypeStruct((pieces, rows, padded), jnp.float32),
-        in_specs=[WHOLE, WHOLE],
-        out_specs=WHOLE,
-        cost_estimate=cost(2 * tokens * depth * width, tokens * padded * 4),
-        compiler_params=pltpu.CompilerParams(vmem_limit_bytes=6 * MIB),
-        name="project",
-    )(section_in, w_down)
 
 
 def norm_rows(pieces, gain, copies):
@@ -103,8 +57,8 @@
 
 def absorb(block_ids, place, slabs, key_up):
     share = len(slabs)
-    _, tokens, _ = slabs[0].shape
-    heads, _, latent = key_up.shape
+    _, query_dim, tokens = slabs[0].shape
+    heads, nope, latent = key_up.shape
     half = tokens // 2
     n_blocks = block_ids.shape[0]
 
@@ -114,14 +68,19 @@
             owner = place_ref[0] + lax.rem(place_ref[1] + share - back, share) * place_ref[2]
             first = (ids_ref[2 * owner] >= n_blocks // 2).astype(jnp.int32)
             for head in range(heads):
-                value = jnp.dot(
-                    slab_ref[head], up_ref[head], preferred_element_type=jnp.float32
+                value = lax.dot_general(
+                    slab_ref[head, :nope],
+                    up_ref[head],
+                    (((0,), (0,)), ((), ())),
+                    preferred_element_type=jnp.float32,
                 ).astype(jnp.bfloat16)
-                rope = slab_ref[heads + head // 2]
-                if head % 2:
-                    rope = jnp.concatenate(
-                        [rope[:, LANES // 2 :], rope[:, : LANES // 2]], axis=-1
-                    )
+                rope = jnp.concatenate(
+                    [
+                        slab_ref[head, nope:].T,
+                        jnp.zeros((tokens, LANES - (query_dim - nope)), jnp.bfloat16),
+                    ],
+                    axis=-1,
+                )
                 rows = pl.ds(head * half, half)
                 out_ref[back, first, rows, :latent] = value[:half]
                 out_ref[back, 1 - first, rows, :latent] = value[half:]
@@ -217,8 +176,8 @@
                 row = pl.multiple_of(receiver * tokens + side * half, half)
                 held[head, pl.ds(row, half), :] = value[span]
                 for at, part in enumerate(parts):
-                    tile = jnp.where(lane == 3 * head + at, part[span], tile)
-            out_ref[receiver, pl.ds(side * half, half), heads * value_dim :] = tile.astype(jnp.bfloat16)
+                    tile = jnp.where(lane == SUBLANES * head + at, part[span], tile)
+            return tile
 
         low_low = masked(0, low_id)
         high_low = score(1, 0)
@@ -234,21 +193,28 @@
         total_high = jnp.sum(high_low, axis=1, keepdims=True) + jnp.sum(
             high_high, axis=1, keepdims=True
         )
-        finish(0, top_low, total_low, weigh(low_low, 0))
-        finish(1, top_high, total_high, weigh(high_low, 0) + weigh(high_high, 1))
+        tiles = (
+            finish(0, top_low, total_low, weigh(low_low, 0)),
+            finish(1, top_high, total_high, weigh(high_low, 0) + weigh(high_high, 1)),
+        )
+        levels = jnp.concatenate(tiles, axis=0).T
+        for head in range(heads):
+            out_ref[receiver, tokens:, head * tokens : (head + 1) * tokens] = levels[
+                head * SUBLANES : (head + 1) * SUBLANES
+            ].astype(jnp.bfloat16)
 
         @pl.when(step == share - 1)
         def _():
             for head in range(heads):
                 value = jnp.dot(held[head], up_ref[head], preferred_element_type=jnp.float32)
-                out_ref[:, :, head * value_dim : (head + 1) * value_dim] = value.astype(
+                out_ref[:, :tokens, head * value_dim : (head + 1) * value_dim] = value.astype(
                     jnp.bfloat16
                 ).reshape(share, tokens, value_dim)
 
-    out_width = heads * value_dim + LANES
+    out_width = heads * value_dim
     return pl.pallas_call(
         kernel,
-        out_shape=jax.ShapeDtypeStruct((share, tokens, out_width), jnp.bfloat16),
+        out_shape=jax.ShapeDtypeStruct((share, tokens + SUBLANES, out_width), jnp.bfloat16),
         grid=(share,),
         in_specs=[
             SCALARS,
@@ -257,7 +223,7 @@
             pl.BlockSpec((sources, tokens, width), lambda g: (0, 0, 0)),
             pl.BlockSpec((heads, latent, value_dim), lambda g: (0, 0, 0)),
         ],
-        out_specs=pl.BlockSpec((share, tokens, out_width), lambda g: (0, 0, 0)),
+        out_specs=pl.BlockSpec((share, tokens + SUBLANES, out_width), lambda g: (0, 0, 0)),
         scratch_shapes=[
             pltpu.VMEM((2, width, n_keys), jnp.bfloat16),
             pltpu.VMEM((2, n_keys, width), jnp.bfloat16),
@@ -273,39 +239,45 @@
 
 
 def combine(block_ids, place, parts, heads):
-    share, tokens, width = parts.shape
-    value_width = width - LANES
-    value_dim = value_width // heads
+    share, rows, width = parts.shape
+    tokens = rows - SUBLANES
+    value_dim = width // heads
     half = tokens // 2
     n_blocks = block_ids.shape[0]
 
     def kernel(ids_ref, place_ref, parts_ref, out_ref):
-        first = (ids_ref[2 * (place_ref[0] + place_ref[1] * place_ref[2])] >= n_blocks // 2).astype(jnp.int32)
+        owner = place_ref[0] + place_ref[1] * place_ref[2]
+        first = (ids_ref[2 * owner] >= n_blocks // 2).astype(jnp.int32)
+        shares = []
+        for head in range(heads):
+            levels = []
+            for k in range(share):
+                stat = parts_ref[k, tokens:, head * tokens : (head + 1) * tokens].astype(
+                    jnp.float32
+                )
+                levels.append(stat[0:1] + stat[1:2] + stat[2:3])
+            top = functools.reduce(jnp.maximum, levels)
+            weights = [jnp.exp2(level - top) for level in levels]
+            inverse = 1.0 / functools.reduce(jnp.add, weights)
+            shares += [weight * inverse for weight in weights]
+        shares += [jnp.zeros((1, tokens), jnp.float32)] * (LANES - len(shares))
+        turned = jnp.concatenate(shares, axis=0).T
         for side in range(2):
             begin = pl.multiple_of(jnp.where(first == side, 0, half), half)
             span = slice(side * half, (side + 1) * half)
-            stats = [parts_ref[k, span, value_width:].astype(jnp.float32) for k in range(share)]
             for head in range(heads):
-                levels = [
-                    s[:, 3 * head : 3 * head + 1]
-                    + s[:, 3 * head + 1 : 3 * head + 2]
-                    + s[:, 3 * head + 2 : 3 * head + 3]
-                    for s in stats
-                ]
-                top = functools.reduce(jnp.maximum, levels)
-                shares = [jnp.exp2(level - top) for level in levels]
-                inverse = 1.0 / functools.reduce(jnp.add, shares)
                 columns = slice(head * value_dim, (head + 1) * value_dim)
                 value = jnp.zeros((half, value_dim), jnp.float32)
                 for k in range(share):
+                    at = head * share + k
                     value += parts_ref[k, span, columns].astype(jnp.float32) * (
-                        shares[k] * inverse
+                        turned[span, at : at + 1]
                     )
                 out_ref[0, pl.ds(begin, half), columns] = value.astype(jnp.bfloat16)
 
     return pl.pallas_call(
         kernel,
-        out_shape=jax.ShapeDtypeStruct((1, tokens, value_width), jnp.bfloat16),
+        out_shape=jax.ShapeDtypeStruct((1, tokens, width), jnp.bfloat16),
         in_specs=[SCALARS, SCALARS, WHOLE],
         out_specs=WHOLE,
         cost_estimate=cost(0, share * tokens * width * 2),
@@ -316,17 +288,26 @@
 
 def shards(outgoing, w_down, kv_gain, queries, w_key_up, w_value_up, block_ids):
     section_idx = lax.axis_index("pp")
+    rows_first = Layout(major_to_minor=(0, 1))
+    hidden = with_layout_constraint(outgoing[0].T, rows_first)
     n_share, n_y0, n_x, tp_size = (lax.axis_size(a) for a in (SHARE, *KEYS, "tp"))
     n_keys = n_y0 * n_x
     tokens, heads, query_dim = queries.shape[1:]
     y1, y0, x = (lax.axis_index(a).astype(jnp.int32) for a in CTX)
     place = jnp.stack([y0 * n_x + x, y1, jnp.int32(n_keys)])
 
-    moved = lax.ppermute(outgoing, "pp", [(0, 1)])
-    section_in = jnp.where(section_idx == 0, outgoing, moved)[0]
-    partial_value = project(section_in, w_down[0], tp_size)
+    moved = with_layout_constraint(lax.ppermute(hidden, "pp", [(0, 1)]), rows_first)
+    section_in = jnp.where(section_idx == 0, hidden, moved)
+    partial_value = lax.dot_general(
+        section_in,
+        w_down[0],
+        (((0,), (0,)), ((), ())),
+        preferred_element_type=jnp.float32,
+    ).reshape(tp_size, tokens // tp_size, -1)
+    spare = -partial_value.shape[-1] % LANES
+    partial_value = jnp.pad(partial_value, ((0, 0), (0, 0), (0, spare)))
     pieces = exchange(partial_value, ("tp",))
-    slabs = [pack_queries(queries[0])]
+    slabs = [queries[0].transpose(1, 2, 0)]
     for ahead in range(1, n_share):
         pairs = [(i, (i + ahead) % n_share) for i in range(n_share)]
         slabs.append(lax.ppermute(slabs[0], SHARE, pairs))

time: 142 us -> 142 us (level)
  the two profiles are of different devices: /device:TPU:72 before, /device:TPU:64 now
where the time goes in v5:
time: 142 us; the launch traced here: 141 us
  blocking collectives  79 us (56%)
  starting transfers between devices  20.9 us (15%)
  waiting for transfers between devices  20.1 us (14%)
  Pallas kernels  11.5 us (8%)
  local copies, waits for them, and re-layouts  8.24 us (6%)
    all_to_all x3, blocking collectives, exchange(): return lax.all_to_all(array, axes, 0, 0, tiled=True)  79 us
    ppermute x3, waiting for transfers between devices, shards(): slabs.append(lax.ppermute(slabs[0], SHARE, pairs))  18.9 us
    ppermute x3, starting transfers between devices, shards(): slabs.append(lax.ppermute(slabs[0], SHARE, pairs))  13.6 us
    pallas_call x1, Pallas kernels, attend(): pl.pallas_call(kernel, out_shape=jax.ShapeDtypeStruct((share, tokens + SU...  8.35 us
    unnamed x24, local copies, waits for them, and re-layouts  6.92 us
    all_to_all x1, starting transfers between devices, exchange(): return lax.all_to_all(array, axes, 0, 0, tiled=True)  5.44 us
  transfers between devices with their start and end apart: 5, of which 3 were waited for; matrix products, arithmetic and copies ran while one was open for 0% of the time, Pallas kernels for 1%

profile of v5, /device:TPU:64, one launch (start us, length us, event | category | flops | bytes accessed | tf_op | source)
XLA Modules:
  0.0 141.1 jit_solution(2017683422954389858)
XLA Ops:
  0.0 1.9 %collective-permute-start.3 = (bf16[448,128]{1,0:T(8,128)(2,1)}, bf16[448,128]{1,0:T(8,128)(2,1)S(1)}, u32[]{:S(2)}, u32[]{:S(2)}) collective-permute-start(bf16[448,128]{1,0:T(8,128)(2,1)} %bitcast.28), channel_id=1, source_target_pairs={{0,16},{1,17},{2,18},{3,19},{4,20},{5,21},{6,22},{7,23},{8,24},{9,... | collective-permute-start | bytes 344072 | tf_op jit(solution)/shard_map/ppermute | solution.py:299
  1.9 1.1 collective-permute-done.3
  3.0 0.9 select_bitcast_fusion
  3.9 0.0 copy-start.9
  4.0 0.1 copy.9
  4.1 0.3 fusion
  4.4 38.8 %all_to_all.20.pieces_ref = f32[16,8,640]{2,1,0:T(8,128)S(1)} all-to-all(f32[16,8,640]{2,1,0:T(8,128)S(1)} %pad.4), channel_id=1, replica_groups=mesh['y1'=4,'y0'=2,'x'=4,'pp'=2,'tp'=16] {'tp'}, dimensions={0} | all-to-all | bytes 655360 | tf_op jit(solution)/shard_map/all_to_all | solution.py:25
  43.2 0.1 norm_rows.1
  43.3 21.8 %all_to_all.21 = bf16[16,8,640]{2,1,0:T(8,128)(2,1)S(1)} all-to-all(bf16[16,8,640]{2,1,0:T(8,128)(2,1)S(1)} %norm_rows.1), channel_id=1, replica_groups=mesh['y1'=4,'y0'=2,'x'=4,'pp'=2,'tp'=16] {'tp'}, dimensions={0} | all-to-all | bytes 327680 | tf_op jit(solution)/shard_map/all_to_all | solution.py:25
  65.0 1.2 broadcast_in_dim.3
  66.2 5.4 %all-to-all-start.2 = ((bf16[8,128,640]{2,1,0:T(8,128)(2,1)}), bf16[8,128,640]{2,1,0:T(8,128)(2,1)}, u32[]{:S(2)}, u32[]{:S(2)}) async-start(bf16[8,128,640]{2,1,0:T(8,128)(2,1)} %broadcast_in_dim.3), calls=%async_computation.2 | async-start | bytes 2621440 | tf_op jit(solution)/shard_map/all_to_all | solution.py:25
  71.7 5.3 %collective-permute-start.2 = (bf16[4,192,128]{2,1,0:T(8,128)(2,1)S(1)}, bf16[4,192,128]{2,1,0:T(8,128)(2,1)S(1)}, u32[]{:S(2)}, u32[]{:S(2)}) collective-permute-start(bf16[4,192,128]{2,1,0:T(8,128)(2,1)S(1)} %bitcast.22), channel_id=1, source_target_pairs={{0,768},{256,0},{512,256},{768,512},{1,769},{257,1},{513,257},{769... | collective-permute-start | bytes 589832 | tf_op jit(solution)/shard_map/ppermute | solution.py:313
  76.9 4.7 %collective-permute-start.1 = (bf16[4,192,128]{2,1,0:T(8,128)(2,1)S(1)}, bf16[4,192,128]{2,1,0:T(8,128)(2,1)S(1)}, u32[]{:S(2)}, u32[]{:S(2)}) collective-permute-start(bf16[4,192,128]{2,1,0:T(8,128)(2,1)S(1)} %bitcast.23), channel_id=1, source_target_pairs={{0,512},{256,768},{512,0},{768,256},{1,513},{257,769},{513,1},{769... | collective-permute-start | bytes 589832 | tf_op jit(solution)/shard_map/ppermute | solution.py:313
  81.7 3.6 %collective-permute-start = (bf16[4,192,128]{2,1,0:T(8,128)(2,1)S(1)}, bf16[4,192,128]{2,1,0:T(8,128)(2,1)S(1)}, u32[]{:S(2)}, u32[]{:S(2)}) collective-permute-start(bf16[4,192,128]{2,1,0:T(8,128)(2,1)S(1)} %bitcast.24), channel_id=1, source_target_pairs={{0,256},{256,512},{512,768},{768,0},{1,257},{257,513},{513,769},{7... | collective-permute-start | bytes 589832 | tf_op jit(solution)/shard_map/ppermute | solution.py:313
  85.3 0.1 pad_add_fusion.place_ref
  85.3 0.0 collective-permute-done.2.refs_3_
  85.4 0.7 copy-done.3
  86.0 18.3 %collective-permute-done.1.refs_2_ = bf16[4,192,128]{2,1,0:T(8,128)(2,1)S(1)} collective-permute-done((bf16[4,192,128]{2,1,0:T(8,128)(2,1)S(1)}, bf16[4,192,128]{2,1,0:T(8,128)(2,1)S(1)}, u32[]{:S(2)}, u32[]{:S(2)}) %collective-permute-start.1) | collective-permute-done | bytes 196640 | tf_op jit(solution)/shard_map/ppermute | solution.py:313
  104.3 0.7 copy-done.5
  105.0 0.6 collective-permute-done.refs_1_
  105.7 0.7 copy-done.7
  106.4 1.0 copy-done.1
  107.4 0.9 copy-done.4
  108.3 0.9 copy-done.6
  109.3 0.9 copy-done.8
  110.2 1.3 absorb.1.query_ref
  111.5 0.0 all-to-all-done.2.keys_ref
  111.5 0.0 copy-start.11
  111.5 1.0 copy-done.11
  112.5 8.4 %attend.1 = bf16[4,136,512]{2,1,0:T(8,128)(2,1)S(1)} custom-call(s32[64]{0:T(128)S(1)} %copy-done.10, s32[3]{0:T(128)S(1)} %pad_add_fusion.place_ref, bf16[4,2,256,640]{3,2,1,0:T(8,128)(2,1)S(1)} %absorb.1.query_ref, bf16[8,128,640]{2,1,0:T(8,128)(2,1)} %all-to-all-done.2.keys_ref, bf16[4,512,128]{2,1,0:T(8,128)(2,1)S(1)} %bitcast.26), custom_call_target="tpu_custom_call" | custom-call | flops 3623878656 | bytes 2621440 | tf_op jit(solution)/shard_map/attend/pallas_call | solution.py:215
  120.9 18.4 %all_to_all.22.parts_ref = bf16[4,136,512]{2,1,0:T(8,128)(2,1)S(1)} all-to-all(bf16[4,136,512]{2,1,0:T(8,128)(2,1)S(1)} %attend.1), channel_id=1, replica_groups=mesh['y1'=4,'y0'=2,'x'=4,'pp'=2,'tp'=16] {'y1'}, dimensions={0} | all-to-all | bytes 1114112 | tf_op jit(solution)/shard_map/all_to_all | solution.py:25
  139.3 1.7 %combine.1 = bf16[1,128,512]{2,1,0:T(8,128)(2,1)} custom-call(s32[64]{0:T(128)S(1)} %copy-done.10, s32[3]{0:T(128)S(1)} %pad_add_fusion.place_ref, bf16[4,136,512]{2,1,0:T(8,128)(2,1)S(1)} %all_to_all.22.parts_ref), custom_call_target="tpu_custom_call" | custom-call | bytes 524288 | tf_op jit(solution)/shard_map/combine/pallas_call | solution.py:278
  (15 shorter events, 0.0 us)
Async XLA Ops:
  0.0 4.1 %copy-start = (bf16[1,448,576]{2,1,0:T(8,128)(2,1)S(1)}, bf16[1,448,576]{2,1,0:T(8,128)(2,1)}, u32[]{:S(2)}) copy-start(bf16[1,448,576]{2,1,0:T(8,128)(2,1)} %param.8) | copy-start | bytes 1548292
  0.0 3.0 %collective-permute-start.3 = (bf16[448,128]{1,0:T(8,128)(2,1)}, bf16[448,128]{1,0:T(8,128)(2,1)S(1)}, u32[]{:S(2)}, u32[]{:S(2)}) collective-permute-start(bf16[448,128]{1,0:T(8,128)(2,1)} %bitcast.28), channel_id=1, source_target_pairs={{0,16},{1,17},{2,18},{3,19},{4,20},{5,21},{6,22},{7,23},{8,24},{9,... | collective-permute-start | bytes 344072 | tf_op jit(solution)/shard_map/ppermute | solution.py:299
  3.9 39.2 %copy-start.9 = (f32[1,512]{1,0:T(1,128)S(1)}, f32[1,512]{1,0:T(1,128)}, u32[]{:S(2)}) copy-start(f32[1,512]{1,0:T(1,128)} %gain_ref.1) | copy-start | bytes 6148
  66.2 5.5 %copy-start.2 = (bf16[1,128,4,192]{1,3,2,0:T(8,128)(2,1)S(1)}, bf16[1,128,4,192]{1,3,2,0:T(8,128)(2,1)}, u32[]{:S(2)}) copy-start(bf16[1,128,4,192]{1,3,2,0:T(8,128)(2,1)} %param.10) | copy-start | bytes 589828
  66.2 40.1 %copy-start.10 = (s32[64]{0:T(128)S(1)}, s32[64]{0:T(128)}, u32[]{:S(2)}) copy-start(s32[64]{0:T(128)} %ids_ref.5) | copy-start | bytes 772
  66.2 45.3 %all-to-all-start.2 = ((bf16[8,128,640]{2,1,0:T(8,128)(2,1)}), bf16[8,128,640]{2,1,0:T(8,128)(2,1)}, u32[]{:S(2)}, u32[]{:S(2)}) async-start(bf16[8,128,640]{2,1,0:T(8,128)(2,1)} %broadcast_in_dim.3), calls=%async_computation.2 | async-start | bytes 2621440 | tf_op jit(solution)/shard_map/all_to_all | solution.py:25
  71.7 13.7 %collective-permute-start.2 = (bf16[4,192,128]{2,1,0:T(8,128)(2,1)S(1)}, bf16[4,192,128]{2,1,0:T(8,128)(2,1)S(1)}, u32[]{:S(2)}, u32[]{:S(2)}) collective-permute-start(bf16[4,192,128]{2,1,0:T(8,128)(2,1)S(1)} %bitcast.22), channel_id=1, source_target_pairs={{0,768},{256,0},{512,256},{768,512},{1,769},{257,1},{513,257},{769... | collective-permute-start | bytes 589832 | tf_op jit(solution)/shard_map/ppermute | solution.py:313
  76.9 27.4 %collective-permute-start.1 = (bf16[4,192,128]{2,1,0:T(8,128)(2,1)S(1)}, bf16[4,192,128]{2,1,0:T(8,128)(2,1)S(1)}, u32[]{:S(2)}, u32[]{:S(2)}) collective-permute-start(bf16[4,192,128]{2,1,0:T(8,128)(2,1)S(1)} %bitcast.23), channel_id=1, source_target_pairs={{0,512},{256,768},{512,0},{768,256},{1,513},{257,769},{513,1},{769... | collective-permute-start | bytes 589832 | tf_op jit(solution)/shard_map/ppermute | solution.py:313
  81.7 24.0 %collective-permute-start = (bf16[4,192,128]{2,1,0:T(8,128)(2,1)S(1)}, bf16[4,192,128]{2,1,0:T(8,128)(2,1)S(1)}, u32[]{:S(2)}, u32[]{:S(2)}) collective-permute-start(bf16[4,192,128]{2,1,0:T(8,128)(2,1)S(1)} %bitcast.24), channel_id=1, source_target_pairs={{0,256},{256,512},{512,768},{768,0},{1,257},{257,513},{513,769},{7... | collective-permute-start | bytes 589832 | tf_op jit(solution)/shard_map/ppermute | solution.py:313
  85.4 0.7 copy-start.3
  104.3 0.7 copy-start.5
  105.7 0.7 copy-start.7
  106.4 1.0 copy-start.1
  107.4 0.9 copy-start.4
  108.3 0.9 copy-start.6
  109.2 0.9 copy-start.8
  111.5 1.0 copy-start.11

commit v6 on v5

--- a/solution.py
+++ b/solution.py
@@ -40,7 +40,8 @@
         latent_part = raw[:, :latent]
         mean_sq = jnp.mean(latent_part * latent_part, axis=-1, keepdims=True)
         normed = latent_part * lax.rsqrt(mean_sq + 1e-06) * gain_ref[...]
-        row = jnp.concatenate([normed, raw[:, latent:]], axis=-1).astype(jnp.bfloat16)
+        spare = jnp.zeros((rows, latent + LANES - width), jnp.float32)
+        row = jnp.concatenate([normed, raw[:, latent:], spare], axis=-1).astype(jnp.bfloat16)
         for copy in range(copies):
             out_ref[copy] = row
 
@@ -112,7 +113,7 @@
     n_keys = sources * half
     factor = scale * LOG2_E
 
-    def kernel(ids_ref, place_ref, query_ref, keys_ref, up_ref, out_ref, turned, plain, held, key_pos):
+    def kernel(ids_ref, place_ref, query_ref, keys_ref, up_ref, out_ref, plain, held, key_pos):
         step = pl.program_id(0)
 
         @pl.when(step == 0)
@@ -136,8 +137,6 @@
             key_pos[0] = low_pos
             low_block = low_pos // half
             key_pos[1] = (n_blocks - 1 - low_block) * half + low_pos % half
-            for side in range(2):
-                turned[side] = plain[side].T
 
         receiver = lax.rem(place_ref[1] + share - step, share)
         id_first = ids_ref[2 * (place_ref[0] + receiver * sources)]
@@ -146,7 +145,12 @@
 
         def score(side, key_side):
             return (
-                jnp.dot(query_ref[0, side], turned[key_side], preferred_element_type=jnp.float32)
+                lax.dot_general(
+                    query_ref[0, side],
+                    plain[key_side],
+                    (((1,), (1,)), ((), ())),
+                    preferred_element_type=jnp.float32,
+                )
                 * factor
             )
 
@@ -225,7 +229,6 @@
         ],
         out_specs=pl.BlockSpec((share, tokens + SUBLANES, out_width), lambda g: (0, 0, 0)),
         scratch_shapes=[
-            pltpu.VMEM((2, width, n_keys), jnp.bfloat16),
             pltpu.VMEM((2, n_keys, width), jnp.bfloat16),
             pltpu.VMEM((heads, share * tokens, latent), jnp.bfloat16),
             pltpu.VMEM((2, 8, n_keys), jnp.int32),
@@ -304,8 +307,6 @@
         (((0,), (0,)), ((), ())),
         preferred_element_type=jnp.float32,
     ).reshape(tp_size, tokens // tp_size, -1)
-    spare = -partial_value.shape[-1] % LANES
-    partial_value = jnp.pad(partial_value, ((0, 0), (0, 0), (0, spare)))
     pieces = exchange(partial_value, ("tp",))
     slabs = [queries[0].transpose(1, 2, 0)]
     for ahead in range(1, n_share):

time: 142 us -> 141 us (level)
  the two profiles are of different devices: /device:TPU:64 before, /device:TPU:74 now
where the time goes in v6:
time: 141 us
  blocking collectives  76.4 us (54%)
  waiting for transfers between devices  22.2 us (16%)
  starting transfers between devices  21.3 us (15%)
  Pallas kernels  11.3 us (8%)
  local copies, waits for them, and re-layouts  8.21 us (6%)
    all_to_all x3, blocking collectives, exchange(): return lax.all_to_all(array, axes, 0, 0, tiled=True)  76.4 us
    ppermute x3, waiting for transfers between devices, shards(): slabs.append(lax.ppermute(slabs[0], SHARE, pairs))  21 us
    ppermute x3, starting transfers between devices, shards(): slabs.append(lax.ppermute(slabs[0], SHARE, pairs))  13.6 us
    pallas_call x1, Pallas kernels, attend(): pl.pallas_call(kernel, out_shape=jax.ShapeDtypeStruct((share, tokens + SU...  8.2 us
    unnamed x24, local copies, waits for them, and re-layouts  6.92 us
    all_to_all x1, starting transfers between devices, exchange(): return lax.all_to_all(array, axes, 0, 0, tiled=True)  5.86 us
  transfers between devices with their start and end apart: 5, of which 3 were waited for; matrix products, arithmetic and copies ran while one was open for 0% of the time, Pallas kernels for 1%

profile of v6, /device:TPU:74, one launch (start us, length us, event | category | flops | bytes accessed | tf_op | source)
XLA Modules:
  0.0 140.8 jit_solution(9546947345882336984)
XLA Ops:
  0.0 0.0 copy-start
  0.0 1.9 %collective-permute-start.3 = (bf16[448,128]{1,0:T(8,128)(2,1)}, bf16[448,128]{1,0:T(8,128)(2,1)S(1)}, u32[]{:S(2)}, u32[]{:S(2)}) collective-permute-start(bf16[448,128]{1,0:T(8,128)(2,1)} %bitcast.28), channel_id=1, source_target_pairs={{0,16},{1,17},{2,18},{3,19},{4,20},{5,21},{6,22},{7,23},{8,24},{9,... | collective-permute-start | bytes 344072 | tf_op jit(solution)/shard_map/ppermute | solution.py:302
  1.9 1.1 collective-permute-done.3
  3.0 0.9 select_bitcast_fusion
  4.0 0.1 copy.9
  4.1 0.3 fusion
  4.4 38.8 %all_to_all.20.pieces_ref = f32[16,8,576]{2,1,0:T(8,128)S(1)} all-to-all(f32[16,8,576]{2,1,0:T(8,128)S(1)} %fusion), channel_id=1, replica_groups=mesh['y1'=4,'y0'=2,'x'=4,'pp'=2,'tp'=16] {'tp'}, dimensions={0} | all-to-all | bytes 589824 | tf_op jit(solution)/shard_map/all_to_all | solution.py:25
  43.1 0.1 norm_rows.1
  43.2 21.8 %all_to_all.21 = bf16[16,8,640]{2,1,0:T(8,128)(2,1)S(1)} all-to-all(bf16[16,8,640]{2,1,0:T(8,128)(2,1)S(1)} %norm_rows.1), channel_id=1, replica_groups=mesh['y1'=4,'y0'=2,'x'=4,'pp'=2,'tp'=16] {'tp'}, dimensions={0} | all-to-all | bytes 327680 | tf_op jit(solution)/shard_map/all_to_all | solution.py:25
  65.0 1.2 broadcast_in_dim.3
  66.2 5.9 %all-to-all-start.2 = ((bf16[8,128,640]{2,1,0:T(8,128)(2,1)}), bf16[8,128,640]{2,1,0:T(8,128)(2,1)}, u32[]{:S(2)}, u32[]{:S(2)}) async-start(bf16[8,128,640]{2,1,0:T(8,128)(2,1)} %broadcast_in_dim.3), calls=%async_computation.2 | async-start | bytes 2621440 | tf_op jit(solution)/shard_map/all_to_all | solution.py:25
  72.0 5.3 %collective-permute-start.2 = (bf16[4,192,128]{2,1,0:T(8,128)(2,1)S(1)}, bf16[4,192,128]{2,1,0:T(8,128)(2,1)S(1)}, u32[]{:S(2)}, u32[]{:S(2)}) collective-permute-start(bf16[4,192,128]{2,1,0:T(8,128)(2,1)S(1)} %bitcast.22), channel_id=1, source_target_pairs={{0,768},{256,0},{512,256},{768,512},{1,769},{257,1},{513,257},{769... | collective-permute-start | bytes 589832 | tf_op jit(solution)/shard_map/ppermute | solution.py:314
  77.3 4.7 %collective-permute-start.1 = (bf16[4,192,128]{2,1,0:T(8,128)(2,1)S(1)}, bf16[4,192,128]{2,1,0:T(8,128)(2,1)S(1)}, u32[]{:S(2)}, u32[]{:S(2)}) collective-permute-start(bf16[4,192,128]{2,1,0:T(8,128)(2,1)S(1)} %bitcast.23), channel_id=1, source_target_pairs={{0,512},{256,768},{512,0},{768,256},{1,513},{257,769},{513,1},{769... | collective-permute-start | bytes 589832 | tf_op jit(solution)/shard_map/ppermute | solution.py:314
  82.0 3.6 %collective-permute-start = (bf16[4,192,128]{2,1,0:T(8,128)(2,1)S(1)}, bf16[4,192,128]{2,1,0:T(8,128)(2,1)S(1)}, u32[]{:S(2)}, u32[]{:S(2)}) collective-permute-start(bf16[4,192,128]{2,1,0:T(8,128)(2,1)S(1)} %bitcast.24), channel_id=1, source_target_pairs={{0,256},{256,512},{512,768},{768,0},{1,257},{257,513},{513,769},{7... | collective-permute-start | bytes 589832 | tf_op jit(solution)/shard_map/ppermute | solution.py:314
  85.6 0.1 pad_add_fusion.place_ref
  85.7 14.0 %collective-permute-done.2.refs_3_ = bf16[4,192,128]{2,1,0:T(8,128)(2,1)S(1)} collective-permute-done((bf16[4,192,128]{2,1,0:T(8,128)(2,1)S(1)}, bf16[4,192,128]{2,1,0:T(8,128)(2,1)S(1)}, u32[]{:S(2)}, u32[]{:S(2)}) %collective-permute-start.2) | collective-permute-done | bytes 196640 | tf_op jit(solution)/shard_map/ppermute | solution.py:314
  99.7 0.7 copy-done.3
  100.4 7.0 %collective-permute-done.1.refs_2_ = bf16[4,192,128]{2,1,0:T(8,128)(2,1)S(1)} collective-permute-done((bf16[4,192,128]{2,1,0:T(8,128)(2,1)S(1)}, bf16[4,192,128]{2,1,0:T(8,128)(2,1)S(1)}, u32[]{:S(2)}, u32[]{:S(2)}) %collective-permute-start.1) | collective-permute-done | bytes 196640 | tf_op jit(solution)/shard_map/ppermute | solution.py:314
  107.4 0.7 copy-done.5
  108.1 0.0 collective-permute-done.refs_1_
  108.1 0.7 copy-done.7
  108.8 1.0 copy-done.1
  109.8 0.9 copy-done.4
  110.8 0.9 copy-done.6
  111.7 0.9 copy-done.8
  112.6 1.3 absorb.1.query_ref
  113.9 0.0 all-to-all-done.2.keys_ref
  113.9 0.0 copy-start.11
  113.9 1.0 copy-done.11
  115.0 8.2 %attend.1 = bf16[4,136,512]{2,1,0:T(8,128)(2,1)S(1)} custom-call(s32[64]{0:T(128)S(1)} %copy-done.10, s32[3]{0:T(128)S(1)} %pad_add_fusion.place_ref, bf16[4,2,256,640]{3,2,1,0:T(8,128)(2,1)S(1)} %absorb.1.query_ref, bf16[8,128,640]{2,1,0:T(8,128)(2,1)} %all-to-all-done.2.keys_ref, bf16[4,512,128]{2,1,0:T(8,128)(2,1)S(1)} %bitcast.26), custom_call_target="tpu_custom_call" | custom-call | flops 3623878656 | bytes 2621440 | tf_op jit(solution)/shard_map/attend/pallas_call | solution.py:219
  123.2 15.9 %all_to_all.22.parts_ref = bf16[4,136,512]{2,1,0:T(8,128)(2,1)S(1)} all-to-all(bf16[4,136,512]{2,1,0:T(8,128)(2,1)S(1)} %attend.1), channel_id=1, replica_groups=mesh['y1'=4,'y0'=2,'x'=4,'pp'=2,'tp'=16] {'y1'}, dimensions={0} | all-to-all | bytes 1114112 | tf_op jit(solution)/shard_map/all_to_all | solution.py:25
  139.1 1.7 %combine.1 = bf16[1,128,512]{2,1,0:T(8,128)(2,1)} custom-call(s32[64]{0:T(128)S(1)} %copy-done.10, s32[3]{0:T(128)S(1)} %pad_add_fusion.place_ref, bf16[4,136,512]{2,1,0:T(8,128)(2,1)S(1)} %all_to_all.22.parts_ref), custom_call_target="tpu_custom_call" | custom-call | bytes 524288 | tf_op jit(solution)/shard_map/combine/pallas_call | solution.py:281
  (14 shorter events, 0.0 us)
Async XLA Ops:
  0.0 4.1 %copy-start = (bf16[1,448,576]{2,1,0:T(8,128)(2,1)S(1)}, bf16[1,448,576]{2,1,0:T(8,128)(2,1)}, u32[]{:S(2)}) copy-start(bf16[1,448,576]{2,1,0:T(8,128)(2,1)} %param.8) | copy-start | bytes 1548292
  0.0 43.1 %copy-start.9 = (f32[1,512]{1,0:T(1,128)S(1)}, f32[1,512]{1,0:T(1,128)}, u32[]{:S(2)}) copy-start(f32[1,512]{1,0:T(1,128)} %gain_ref.1) | copy-start | bytes 6148
  0.0 3.0 %collective-permute-start.3 = (bf16[448,128]{1,0:T(8,128)(2,1)}, bf16[448,128]{1,0:T(8,128)(2,1)S(1)}, u32[]{:S(2)}, u32[]{:S(2)}) collective-permute-start(bf16[448,128]{1,0:T(8,128)(2,1)} %bitcast.28), channel_id=1, source_target_pairs={{0,16},{1,17},{2,18},{3,19},{4,20},{5,21},{6,22},{7,23},{8,24},{9,... | collective-permute-start | bytes 344072 | tf_op jit(solution)/shard_map/ppermute | solution.py:302
  66.2 5.9 %copy-start.2 = (bf16[1,128,4,192]{1,3,2,0:T(8,128)(2,1)S(1)}, bf16[1,128,4,192]{1,3,2,0:T(8,128)(2,1)}, u32[]{:S(2)}) copy-start(bf16[1,128,4,192]{1,3,2,0:T(8,128)(2,1)} %param.10) | copy-start | bytes 589828
  66.2 42.6 %copy-start.10 = (s32[64]{0:T(128)S(1)}, s32[64]{0:T(128)}, u32[]{:S(2)}) copy-start(s32[64]{0:T(128)} %ids_ref.5) | copy-start | bytes 772
  66.2 47.7 %all-to-all-start.2 = ((bf16[8,128,640]{2,1,0:T(8,128)(2,1)}), bf16[8,128,640]{2,1,0:T(8,128)(2,1)}, u32[]{:S(2)}, u32[]{:S(2)}) async-start(bf16[8,128,640]{2,1,0:T(8,128)(2,1)} %broadcast_in_dim.3), calls=%async_computation.2 | async-start | bytes 2621440 | tf_op jit(solution)/shard_map/all_to_all | solution.py:25
  72.0 27.7 %collective-permute-start.2 = (bf16[4,192,128]{2,1,0:T(8,128)(2,1)S(1)}, bf16[4,192,128]{2,1,0:T(8,128)(2,1)S(1)}, u32[]{:S(2)}, u32[]{:S(2)}) collective-permute-start(bf16[4,192,128]{2,1,0:T(8,128)(2,1)S(1)} %bitcast.22), channel_id=1, source_target_pairs={{0,768},{256,0},{512,256},{768,512},{1,769},{257,1},{513,257},{769... | collective-permute-start | bytes 589832 | tf_op jit(solution)/shard_map/ppermute | solution.py:314
  77.3 30.1 %collective-permute-start.1 = (bf16[4,192,128]{2,1,0:T(8,128)(2,1)S(1)}, bf16[4,192,128]{2,1,0:T(8,128)(2,1)S(1)}, u32[]{:S(2)}, u32[]{:S(2)}) collective-permute-start(bf16[4,192,128]{2,1,0:T(8,128)(2,1)S(1)} %bitcast.23), channel_id=1, source_target_pairs={{0,512},{256,768},{512,0},{768,256},{1,513},{257,769},{513,1},{769... | collective-permute-start | bytes 589832 | tf_op jit(solution)/shard_map/ppermute | solution.py:314
  82.0 26.1 %collective-permute-start = (bf16[4,192,128]{2,1,0:T(8,128)(2,1)S(1)}, bf16[4,192,128]{2,1,0:T(8,128)(2,1)S(1)}, u32[]{:S(2)}, u32[]{:S(2)}) collective-permute-start(bf16[4,192,128]{2,1,0:T(8,128)(2,1)S(1)} %bitcast.24), channel_id=1, source_target_pairs={{0,256},{256,512},{512,768},{768,0},{1,257},{257,513},{513,769},{7... | collective-permute-start | bytes 589832 | tf_op jit(solution)/shard_map/ppermute | solution.py:314
  99.7 0.7 copy-start.3
  107.4 0.7 copy-start.5
  108.1 0.7 copy-start.7
  108.8 1.0 copy-start.1
  109.8 0.9 copy-start.4
  110.8 0.9 copy-start.6
  111.7 0.9 copy-start.8
  113.9 1.0 copy-start.11
